TPU v7x, 32 devices: a whole 2x2x4 slice. The times are simulated.
32 devices in a mesh: panel: 2 (over y), row: 4 (over z), layer: 4 (over x, core).
Axes of the slice: x: 2, y: 2, z: 4, core: 2. Of those that a mesh axis runs over, the one named last changes fastest.
Arguments:
- layers: bfloat16 [4, 8192, 512], P('layer', 'row', 'panel'), parts along dimension 2, may hold values from -6 to 6
- table: bfloat16 [16, 128, 64], replicated, may hold values from -0.375 to 0.375
- fitting: bfloat16 [8192, 6600], P('row', 'layer'), may hold values from -0.09375 to 0.09375
- owner: int32 [4, 128, 1], P('layer', 'row'), may hold values from 0 to 3; in each aligned block of 32 rows (0 to 31, 32 to 63, ..., all dimensions but the last counted through in order) at most 16 rows name the same one
- local_slice: int32 [4, 128], P('layer', 'row'), may hold values from 0 to 15
- block_index: int32 [4, 128], P('layer', 'row'), may hold values from 0 to 31
- weight_index: int32 [4, 128], P('layer', 'row'), may hold values from 0 to 15
Outputs:
- actuators: bfloat16 [512, 6600], P(('panel', 'row'), 'layer'), parts along dimension 0
There are 2 independent parts, one for each index of `panel`. A program takes and returns all parts, laid end to end along the dimension named above; an argument that names none is the same for every part. Nothing has to cross between parts.
Inputs may be any that keep to these rules, and one draw needn't show every extreme that they name: `owner`: within the 32 entries of one layer on one row device (aligned blocks of 32 entries), no value is named more than 16 times, and in every draw some block names one value exactly 16 times.
All inputs are finite; a program needn't handle non-finite values.
Results may differ from a plain program's by a relative error of at most 0.0058.
Values may be sent and summed in bfloat16 or wider, within the bound.
A program may use at most 64 MiB of HBM per device.

v0:
```python
import functools

import jax
import jax.numpy as jnp
from jax import lax
from jax.experimental import pallas as pl
from jax.experimental.pallas import tpu as pltpu

MESH = pl.DeviceIdType.MESH
from jax.sharding import PartitionSpec as P


def local_rows(layers, table, fitting, owner, local_slice, block_index, weight_index):
    rows_dev = layers.shape[1]
    columns = layers.shape[2]
    slice_rows = table.shape[1]
    block_rows = table.shape[2]
    entries = owner.shape[1]
    peer_count = lax.axis_size("row")
    capacity = max(2, 2 * entries // peer_count)
    slot_count = peer_count * capacity
    owned_slices = fitting.shape[0] // slice_rows
    owner_now = owner[0, :, 0]
    local_now = local_slice[0]
    owner_match = (owner_now[:, None] == jnp.arange(peer_count, dtype=jnp.int32)[None, :]).astype(
        jnp.int32
    )
    slot_rank = jnp.sum((jnp.cumsum(owner_match, axis=0) - 1) * owner_match, axis=1)
    target = owner_now * capacity + slot_rank
    placed = target[None, :] == jnp.arange(slot_count, dtype=jnp.int32)[:, None]
    filled = jnp.any(placed, axis=1)
    source = jnp.sum(jnp.where(placed, jnp.arange(entries, dtype=jnp.int32)[None, :], 0), axis=1)
    send_local = jnp.where(filled, local_now[source], -1).reshape(peer_count, capacity)
    grouped = layers[0].reshape(rows_dev // block_rows, block_rows, columns)
    picked = grouped[block_index[0][source]].reshape(peer_count, capacity, block_rows, columns)
    send_weight = weight_index[0][source].reshape(peer_count, capacity)
    got_rows, got_weight, got_local = (
        lax.all_to_all(picked, "row", split_axis=0, concat_axis=0, tiled=True),
        lax.all_to_all(send_weight, "row", split_axis=0, concat_axis=0, tiled=True),
        lax.all_to_all(send_local, "row", split_axis=0, concat_axis=0, tiled=True),
    )
    pupil_terms = jnp.einsum(
        "ksb,kbc->ksc",
        table[got_weight.reshape(-1)],
        got_rows.reshape(slot_count, block_rows, columns),
        preferred_element_type=jnp.float32,
    ).astype(jnp.bfloat16)
    selector = (
        jnp.arange(owned_slices, dtype=jnp.int32)[:, None] == got_local.reshape(-1)[None, :]
    ).astype(jnp.bfloat16)
    partial_pupil = jnp.dot(
        selector,
        pupil_terms.reshape(slot_count, slice_rows * columns),
        preferred_element_type=jnp.float32,
    ).reshape(owned_slices * slice_rows, columns)
    pupil_rounded = lax.psum(partial_pupil, "layer").astype(jnp.bfloat16)
    return lax.psum_scatter(
        lax.dot_general(
            pupil_rounded, fitting, (((0,), (0,)), ((), ())), preferred_element_type=jnp.float32
        ),
        "row",
        scatter_dimension=0,
        tiled=True,
    ).astype(jnp.bfloat16)


def swap_kernel(
    rows_ref, meta_ref, turned_ref, got_ref, got_meta_ref, table_ref, send_sem, recv_sem
):
    me = lax.axis_index("layer")
    half = got_ref.shape[1]
    partner = lax.rem(me + 2, 4)
    barrier = pltpu.get_barrier_semaphore()
    pl.semaphore_signal(barrier, inc=1, device_id={"layer": partner}, device_id_type=MESH)
    pl.semaphore_wait(barrier, 1)
    first = pl.multiple_of((1 - me // 2) * half, half)
    copies = [
        pltpu.make_async_remote_copy(
            src_ref=source,
            dst_ref=target,
            send_sem=send_sem.at[index],
            recv_sem=recv_sem.at[index],
            device_id={"layer": partner},
            device_id_type=MESH,
        )
        for index, (source, target) in enumerate(
            ((meta_ref, got_meta_ref), (rows_ref.at[:, pl.ds(first, half)], got_ref))
        )
    ]
    for copy in copies:
        copy.start()
    for index in range(table_ref.shape[0]):
        table_ref[index] = turned_ref[index].T
    for copy in copies:
        copy.wait()


def swap(rows, meta, table):
    any_space = pl.BlockSpec(memory_space=pl.ANY)
    vmem = pl.BlockSpec(memory_space=pltpu.VMEM)
    return pl.pallas_call(
        swap_kernel,
        out_shape=(
            jax.ShapeDtypeStruct((rows.shape[0], rows.shape[1] // 2), rows.dtype),
            jax.ShapeDtypeStruct(meta.shape, meta.dtype),
            jax.ShapeDtypeStruct(table.shape, table.dtype),
        ),
        in_specs=[any_space, any_space, vmem],
        out_specs=(any_space, any_space, vmem),
        scratch_shapes=[pltpu.SemaphoreType.DMA((2,)), pltpu.SemaphoreType.DMA((2,))],
        compiler_params=pltpu.CompilerParams(collective_id=1, has_side_effects=True),
    )(rows, meta, table.transpose(0, 2, 1))


def terms_kernel(
    peers, half_slices, own_ref, got_ref, table_ref, meta_ref, got_meta_ref, out_ref, total_ref
):
    entries = meta_ref.shape[1]
    block_rows = table_ref.shape[2]
    half = got_ref.shape[1]
    first = pl.multiple_of(lax.axis_index("layer") // 2 * half, half)
    total_ref[...] = jnp.zeros_like(total_ref)
    group = 16 if entries % 16 == 0 else 1
    for index_ref, rows_ref, lanes in (
        (meta_ref, own_ref, pl.ds(first, half)),
        (got_meta_ref, got_ref, slice(None)),
    ):

        def step(index, carry):
            terms = []
            for offset in range(group):
                entry = index * group + offset
                start = pl.multiple_of(index_ref[2, entry] * block_rows, block_rows)
                terms.append(
                    jnp.dot(
                        table_ref[index_ref[3, entry]],
                        rows_ref[pl.ds(start, block_rows), lanes],
                        preferred_element_type=jnp.float32,
                    )
                )
            for offset in range(group):
                entry = index * group + offset
                local_now = index_ref[1, entry]
                upper = (local_now >= half_slices).astype(jnp.int32)
                place = (upper * (peers - 1) + index_ref[0, entry]) * half_slices + local_now
                total_ref[place] += terms[offset]
            return carry

        lax.fori_loop(0, entries // group, step, 0)

    def write(index, carry):
        out_ref[index] = total_ref[index].astype(out_ref.dtype)
        return carry

    lax.fori_loop(0, out_ref.shape[0], write, 0, unroll=4)


def exchange_kernel(
    peers, part_ref, fitting_ref, out_ref,
    fit, core_in, both, row_in, pieces, total, product, landed,
    fit_sem, core_send, core_recv, row_send, row_recv, layer_send, layer_recv, end_send, end_recv,
):
    row = lax.axis_index("row")
    me = lax.axis_index("layer")
    core = lax.rem(me, 2)
    steps = core_send.shape[0]
    piece_rows = pieces.shape[1]
    rows = piece_rows // steps
    width = fit.shape[0]
    half_columns = pieces.shape[2]
    out_rows = out_ref.shape[0]
    mate = row + 1 - 2 * lax.rem(row, 2)
    cross = lax.rem(row + 2, peers)
    opposite = peers - 1 - row
    is_end = jnp.logical_or(row == 0, row == peers - 1)
    is_middle = jnp.logical_not(is_end)
    layer_peers = [lax.rem(me + k, 4) for k in range(1, 4)]

    fit_copy = pltpu.make_async_copy(fitting_ref, fit, fit_sem)
    fit_copy.start()
    barrier = pltpu.get_barrier_semaphore()
    for peer in (mate, cross, opposite):
        pl.semaphore_signal(barrier, inc=1, device_id={"row": peer}, device_id_type=MESH)
    for peer in layer_peers:
        pl.semaphore_signal(barrier, inc=1, device_id={"layer": peer}, device_id_type=MESH)
    pl.semaphore_wait(barrier, peers - 1 + 3)

    core_copies = []
    for step in range(steps):
        copy = pltpu.make_async_remote_copy(
            src_ref=part_ref.at[1 - core, :, pl.ds(step * rows, rows), :],
            dst_ref=core_in.at[:, pl.ds(step * rows, rows), :],
            send_sem=core_send.at[step],
            recv_sem=core_recv.at[step],
            device_id={"layer": me + 1 - 2 * core},
            device_id_type=MESH,
        )
        copy.start()
        core_copies.append(copy)

    def row_copy(slot, step, source, peer):
        part = pl.ds(step * rows, rows)
        return pltpu.make_async_remote_copy(
            src_ref=both.at[source, part, :],
            dst_ref=row_in.at[slot, part, :],
            send_sem=row_send.at[slot, step],
            recv_sem=row_recv.at[slot, step],
            device_id={"row": peer},
            device_id_type=MESH,
        )

    for step in range(steps):
        part = slice(step * rows, (step + 1) * rows)
        core_copies[step].wait_recv()
        both[:, part, :] = (
            part_ref[core, :, part, :].astype(jnp.float32) + core_in[:, part, :].astype(jnp.float32)
        ).astype(both.dtype)

        @pl.when(is_end)
        def _():
            row_copy(3, step, opposite, mate).start()
            row_copy(1, step, cross, cross).start()

        @pl.when(is_middle)
        def _():
            row_copy(2, step, opposite, opposite).start()

        row_copy(0, step, mate, mate).start()

    def join(step):
        part = slice(step * rows, (step + 1) * rows)

        @pl.when(is_middle)
        def _():
            row_copy(3, step, opposite, mate).wait_recv()
            both[cross, part, :] = (
                both[cross, part, :].astype(jnp.float32) + row_in[3, part, :].astype(jnp.float32)
            ).astype(both.dtype)
            row_copy(1, step, cross, cross).start()

    tiles = [(start, min(start + 512, width)) for start in range(0, width, 512)]

    def multiply(step):
        for start, stop in tiles:
            value = None
            for half in range(2):
                part = slice(step * rows, (step + 1) * rows)
                left = jnp.concatenate([pieces[half, part, :], pieces[2 + half, part, :]], axis=1)
                first = half * piece_rows + step * rows
                term = lax.dot_general(
                    left,
                    fit[start:stop, first : first + rows],
                    (((0,), (1,)), ((), ())),
                    preferred_element_type=jnp.float32,
                )
                value = term if value is None else value + term
            if step == 0:
                total[:, start:stop] = value
            else:
                total[:, start:stop] += value

    layer_copies = []
    join(0)
    for step in range(steps):
        part = slice(step * rows, (step + 1) * rows)
        row_copy(0, step, mate, mate).wait_recv()
        row_copy(1, step, cross, cross).wait_recv()

        @pl.when(is_end)
        def _():
            value = both[row, part, :].astype(jnp.float32)
            for slot in range(2):
                value = value + row_in[slot, part, :].astype(jnp.float32)
            pieces[me, part, :] = value.astype(pieces.dtype)

        @pl.when(is_middle)
        def _():
            row_copy(2, step, opposite, opposite).wait_recv()
            value = both[row, part, :].astype(jnp.float32)
            for slot in range(3):
                value = value + row_in[slot, part, :].astype(jnp.float32)
            pieces[me, part, :] = value.astype(pieces.dtype)

        sent = []
        for k, peer in enumerate(layer_peers):
            copy = pltpu.make_async_remote_copy(
                src_ref=pieces.at[me, pl.ds(step * rows, rows), :],
                dst_ref=pieces.at[me, pl.ds(step * rows, rows), :],
                send_sem=layer_send.at[k, step],
                recv_sem=layer_recv.at[k, step],
                device_id={"layer": peer},
                device_id_type=MESH,
            )
            copy.start()
            sent.append(copy)
        layer_copies.append(sent)
        if step + 1 < steps:
            join(step + 1)
        if step == 0:
            fit_copy.wait()
        if step > 0:
            for copy in layer_copies[step - 1]:
                copy.wait_recv()
            multiply(step - 1)
    for copy in layer_copies[steps - 1]:
        copy.wait_recv()
    multiply(steps - 1)

    padded = product.shape[2]
    pieces_out = end_send.shape[1]
    cuts = [padded // 128 * cut // pieces_out * 128 for cut in range(pieces_out + 1)]
    if width < padded:
        product[:, :, padded - 128 :] = jnp.zeros((peers, out_rows, 128), product.dtype)

    def end_copy(slot, cut, source, peer):
        span = pl.ds(cuts[cut], cuts[cut + 1] - cuts[cut])
        return pltpu.make_async_remote_copy(
            src_ref=product.at[source, :, span],
            dst_ref=landed.at[slot, :, span],
            send_sem=end_send.at[slot, cut],
            recv_sem=end_recv.at[slot, cut],
            device_id={"row": peer},
            device_id_type=MESH,
        )

    def lanes_of(cut):
        return slice(cuts[cut], min(cuts[cut + 1], width))

    def total_of(owner, lanes):
        return total[pl.ds(pl.multiple_of(owner * out_rows, out_rows), out_rows), lanes]

    for cut in range(pieces_out):
        lanes = lanes_of(cut)

        @pl.when(is_end)
        def _():
            for peer in (opposite, cross, mate):
                product[peer, :, lanes] = total_of(peer, lanes).astype(product.dtype)
            end_copy(3, cut, opposite, mate).start()
            end_copy(1, cut, cross, cross).start()
            end_copy(0, cut, mate, mate).start()

        @pl.when(is_middle)
        def _():
            for peer in (opposite, mate):
                product[peer, :, lanes] = total_of(peer, lanes).astype(product.dtype)
            end_copy(2, cut, opposite, opposite).start()
            end_copy(0, cut, mate, mate).start()

    @pl.when(is_middle)
    def _():
        for cut in range(pieces_out):
            lanes = lanes_of(cut)
            end_copy(3, cut, opposite, mate).wait_recv()
            product[cross, :, lanes] = (
                total_of(cross, lanes) + landed[3, :, lanes].astype(jnp.float32)
            ).astype(product.dtype)
            end_copy(1, cut, cross, cross).start()

    for cut in range(pieces_out):
        lanes = lanes_of(cut)
        end_copy(0, cut, mate, mate).wait_recv()
        end_copy(1, cut, cross, cross).wait_recv()

        @pl.when(is_end)
        def _():
            value = total_of(row, lanes)
            for slot in range(2):
                value = value + landed[slot, :, lanes].astype(jnp.float32)
            out_ref[:, lanes] = value.astype(out_ref.dtype)

        @pl.when(is_middle)
        def _():
            end_copy(2, cut, opposite, opposite).wait_recv()
            value = total_of(row, lanes)
            for slot in range(3):
                value = value + landed[slot, :, lanes].astype(jnp.float32)
            out_ref[:, lanes] = value.astype(out_ref.dtype)

    for copy in core_copies:
        copy.wait_send()
    for sent in layer_copies:
        for copy in sent:
            copy.wait_send()

    def finish(copy_of, count):
        for index in range(count):
            copy_of(0, index, mate, mate).wait_send()
            copy_of(1, index, cross, cross).wait_send()

            @pl.when(is_end)
            def _():
                copy_of(3, index, opposite, mate).wait_send()

            @pl.when(is_middle)
            def _():
                copy_of(2, index, opposite, opposite).wait_send()

    finish(row_copy, steps)
    finish(end_copy, pieces_out)


def exchange(partial, fitting):
    _, peers, piece_rows, half_columns = partial.shape
    depth, width = fitting.shape
    columns = 2 * half_columns
    out_rows = columns // peers
    padded = -(-width // 128) * 128
    steps = 4
    dma = pltpu.SemaphoreType.DMA
    return pl.pallas_call(
        functools.partial(exchange_kernel, peers),
        out_shape=jax.ShapeDtypeStruct((out_rows, width), jnp.bfloat16),
        in_specs=[pl.BlockSpec(memory_space=pltpu.VMEM), pl.BlockSpec(memory_space=pl.ANY)],
        out_specs=pl.BlockSpec(memory_space=pltpu.VMEM),
        scratch_shapes=[
            pltpu.VMEM((width, depth), jnp.bfloat16),
            pltpu.VMEM((peers, piece_rows, half_columns), jnp.bfloat16),
            pltpu.VMEM((peers, piece_rows, half_columns), jnp.bfloat16),
            pltpu.VMEM((4, piece_rows, half_columns), jnp.bfloat16),
            pltpu.VMEM((4, piece_rows, half_columns), jnp.bfloat16),
            pltpu.VMEM((columns, width), jnp.float32),
            pltpu.VMEM((peers, out_rows, padded), jnp.bfloat16),
            pltpu.VMEM((4, out_rows, padded), jnp.bfloat16),
            dma,
            dma((steps,)),
            dma((steps,)),
            dma((4, steps)),
            dma((4, steps)),
            dma((3, steps)),
            dma((3, steps)),
            dma((4, 3)),
            dma((4, 3)),
        ],
        compiler_params=pltpu.CompilerParams(collective_id=0, has_side_effects=True),
    )(partial, fitting.T)


def local_reduced(layers, table, fitting, owner, local_slice, block_index, weight_index):
    columns = layers.shape[2]
    slice_rows = table.shape[1]
    peer_count = lax.axis_size("row")
    owned_slices = fitting.shape[0] // slice_rows
    half_slices = owned_slices // 2
    half_columns = columns // 2
    slice_total = peer_count * owned_slices
    meta = jnp.stack([owner[0, :, 0], local_slice[0], block_index[0], weight_index[0]])
    got, got_meta, turned = swap(layers[0], meta, table)
    partial = pl.pallas_call(
        functools.partial(terms_kernel, peer_count, half_slices),
        out_shape=jax.ShapeDtypeStruct((slice_total, slice_rows, half_columns), jnp.bfloat16),
        in_specs=[pl.BlockSpec(memory_space=pltpu.VMEM)] * 3
        + [pl.BlockSpec(memory_space=pltpu.SMEM)] * 2,
        out_specs=pl.BlockSpec(memory_space=pltpu.VMEM),
        scratch_shapes=[pltpu.VMEM((slice_total, slice_rows, half_columns), jnp.float32)],
    )(layers[0], got, turned, meta, got_meta)
    partial = partial.reshape(2, peer_count, half_slices * slice_rows, half_columns)
    return exchange(partial, fitting)


def local(layers, table, fitting, owner, local_slice, block_index, weight_index):
    arguments = (layers, table, fitting, owner, local_slice, block_index, weight_index)
    entries, peers, group = owner.shape[1], lax.axis_size("row"), lax.axis_size("layer")
    raw_rows = max(2, 2 * entries // peers) * table.shape[2]
    reduced_rows = fitting.shape[0] // group
    if group == 4 and peers == 4 and raw_rows > reduced_rows:
        return local_reduced(*arguments)
    return local_rows(*arguments)


def solution(mesh):
    return jax.shard_map(
        local,
        mesh=mesh,
        in_specs=(
            P("layer", "row", "panel"),
            P(),
            P("row", "layer"),
            P("layer", "row", None),
            P("layer", "row"),
            P("layer", "row"),
            P("layer", "row"),
        ),
        out_specs=P(("panel", "row"), "layer"),
        check_vma=False,
    )
```

profile of v0, /device:TPU:0, one launch (start us, length us, event | category | flops | bytes accessed | tf_op | source)
XLA Modules:
  0.0 74.0 jit_solution(12650870593379600485)
XLA Ops:
  0.0 1.3 %pad_add_fusion.meta_ref = s32[4,32]{1,0:T(4,128)} fusion(s32[1,32]{1,0:T(1,128)} %param.13, s32[1,32]{1,0:T(1,128)} %param.12, s32[1,32]{1,0:T(1,128)} %param.11, s32[1,32]{1,0:T(1,128)} %bitcast.10), kind=kLoop, calls=%fused_computation | loop fusion | flops 384 | bytes 1024 | tf_op jit(solution)/shard_map/stack | solution.py:447
  1.3 17.0 %shard_map.73 = (bf16[2048,128]{1,0:T(8,128)(2,1)}, s32[4,32]{1,0:T(4,128)}, bf16[16,128,64]{2,1,0:T(8,128)(2,1)}) custom-call(bf16[2048,256]{1,0:T(8,128)(2,1)} %bitcast.7, s32[4,32]{1,0:T(4,128)} %pad_add_fusion.meta_ref, bf16[16,64,128]{2,1,0:T(8,128)(2,1)} %bitcast.9), custom_call_target="tpu_custom_call" | custom-call | tf_op jit(solution)/shard_map/pallas_call | solution.py:101
  18.3 4.6 %shard_map.74 = bf16[64,128,128]{2,1,0:T(8,128)(2,1)} custom-call(bf16[2048,256]{1,0:T(8,128)(2,1)} %bitcast.8, bf16[2048,128]{1,0:T(8,128)(2,1)} %get-tuple-element.8.got_ref, bf16[16,128,64]{2,1,0:T(8,128)(2,1)} %get-tuple-element.9.table_ref, s32[4,32]{1,0:T(4,128)} %pad_add_fusion.meta_ref, s32[4,32]{1,0:T(4,128)} %get-tuple-element.10.got_meta_ref), custom_call_target="tpu_custom_call" | custom-call | tf_op jit(solution)/shard_map/pallas_call | solution.py:449
  23.0 49.4 %shard_map.75 = bf16[64,1650]{1,0:T(8,128)(2,1)} custom-call(bf16[2,4,1024,128]{3,2,1,0:T(8,128)(2,1)} %bitcast.5, bf16[1650,2048]{1,0:T(8,128)(2,1)} %bitcast.6), custom_call_target="tpu_custom_call" | custom-call | tf_op jit(solution)/shard_map/pallas_call | solution.py:411
  72.4 1.6 %copy.9 = bf16[64,1650]{1,0:T(8,128)(2,1)} copy(bf16[64,1650]{1,0:T(8,128)(2,1)} %shard_map.75) | data formatting | bytes 422400
where the time goes:
time: 74.3 us; the launch traced here: 74 us
  Pallas kernels  71.1 us (96%)
  local copies, waits for them, and re-layouts  1.63 us (2%)
  other arithmetic  1.29 us (2%)
    pallas_call x1, Pallas kernels, exchange(): pl.pallas_call(functools.partial(exchange_kernel, peers), out_shape=jax.S...  49.4 us
    pallas_call x1, Pallas kernels, swap(): pl.pallas_call(swap_kernel, out_shape=(jax.ShapeDtypeStruct((rows.shape[0...  17 us
    pallas_call x1, Pallas kernels, local_reduced(): pl.pallas_call(functools.partial(terms_kernel, peer_count, half_slices),...  4.61 us
    unnamed x1, local copies, waits for them, and re-layouts  1.63 us

commit v1 on v0

v1 whole, which is shorter than its diff:
```python
import functools

import jax
import jax.numpy as jnp
from jax import lax
from jax.experimental import pallas as pl
from jax.experimental.pallas import tpu as pltpu

MESH = pl.DeviceIdType.MESH
from jax.sharding import PartitionSpec as P


def local_rows(layers, table, fitting, owner, local_slice, block_index, weight_index):
    rows_dev = layers.shape[1]
    columns = layers.shape[2]
    slice_rows = table.shape[1]
    block_rows = table.shape[2]
    entries = owner.shape[1]
    peer_count = lax.axis_size("row")
    capacity = max(2, 2 * entries // peer_count)
    slot_count = peer_count * capacity
    owned_slices = fitting.shape[0] // slice_rows
    owner_now = owner[0, :, 0]
    local_now = local_slice[0]
    owner_match = (owner_now[:, None] == jnp.arange(peer_count, dtype=jnp.int32)[None, :]).astype(
        jnp.int32
    )
    slot_rank = jnp.sum((jnp.cumsum(owner_match, axis=0) - 1) * owner_match, axis=1)
    target = owner_now * capacity + slot_rank
    placed = target[None, :] == jnp.arange(slot_count, dtype=jnp.int32)[:, None]
    filled = jnp.any(placed, axis=1)
    source = jnp.sum(jnp.where(placed, jnp.arange(entries, dtype=jnp.int32)[None, :], 0), axis=1)
    send_local = jnp.where(filled, local_now[source], -1).reshape(peer_count, capacity)
    grouped = layers[0].reshape(rows_dev // block_rows, block_rows, columns)
    picked = grouped[block_index[0][source]].reshape(peer_count, capacity, block_rows, columns)
    send_weight = weight_index[0][source].reshape(peer_count, capacity)
    got_rows, got_weight, got_local = (
        lax.all_to_all(picked, "row", split_axis=0, concat_axis=0, tiled=True),
        lax.all_to_all(send_weight, "row", split_axis=0, concat_axis=0, tiled=True),
        lax.all_to_all(send_local, "row", split_axis=0, concat_axis=0, tiled=True),
    )
    pupil_terms = jnp.einsum(
        "ksb,kbc->ksc",
        table[got_weight.reshape(-1)],
        got_rows.reshape(slot_count, block_rows, columns),
        preferred_element_type=jnp.float32,
    ).astype(jnp.bfloat16)
    selector = (
        jnp.arange(owned_slices, dtype=jnp.int32)[:, None] == got_local.reshape(-1)[None, :]
    ).astype(jnp.bfloat16)
    partial_pupil = jnp.dot(
        selector,
        pupil_terms.reshape(slot_count, slice_rows * columns),
        preferred_element_type=jnp.float32,
    ).reshape(owned_slices * slice_rows, columns)
    pupil_rounded = lax.psum(partial_pupil, "layer").astype(jnp.bfloat16)
    return lax.psum_scatter(
        lax.dot_general(
            pupil_rounded, fitting, (((0,), (0,)), ((), ())), preferred_element_type=jnp.float32
        ),
        "row",
        scatter_dimension=0,
        tiled=True,
    ).astype(jnp.bfloat16)


def index_table(owner, local_slice, block, weight, owned, weights, slices, out_ref):
    entries = owner.shape[1]
    square = (entries, entries)
    down = lax.broadcasted_iota(jnp.int32, square, 0)
    along = lax.broadcasted_iota(jnp.int32, square, 1)

    def upright(row):
        return jnp.sum(jnp.where(down == along, jnp.broadcast_to(row, square), 0), axis=1, keepdims=True)

    place = owner * owned + local_slice
    place_up = upright(place)
    place_row = jnp.broadcast_to(place, square)
    twin = (place_row == place_up) & (along < down)
    rank = jnp.sum(((place_row < place_up) | twin).astype(jnp.int32), axis=1, keepdims=True)
    follows = (jnp.sum(twin.astype(jnp.int32), axis=1, keepdims=True) > 0).astype(jnp.int32)
    code = upright(block * weights + weight)
    moved = rank == along
    code = jnp.sum(jnp.where(moved, jnp.broadcast_to(code, square), 0), axis=0, keepdims=True)
    follows = jnp.sum(jnp.where(moved, jnp.broadcast_to(follows, square), 0), axis=0, keepdims=True)
    names = lax.broadcasted_iota(jnp.int32, (entries, slices), 1)
    place_wide = jnp.broadcast_to(place_up, (entries, slices))
    until = jnp.sum((place_wide <= names).astype(jnp.int32), axis=0, keepdims=True)
    held = jnp.sum((place_wide == names).astype(jnp.int32), axis=0, keepdims=True)
    block = code // weights
    out_ref[0:1, 0:entries] = block // 2
    out_ref[1:2, 0:entries] = (block % 2) * weights + code % weights
    out_ref[2:3, 0:entries] = follows
    out_ref[3:4, 0:slices] = jnp.where(held > 0, until, 0)


def fused_kernel(
    peers, owned, spans,
    layers_ref, turned_ref, owner_ref, local_ref, block_ref, weight_ref, fitting_ref, out_ref,
    other_raw, own_raw, own_turned, wide_table, own_sums, got_sums, meta, own_index, got_index,
    fit, left, total, own_part, chunk_refs,
    in_sem, meta_sem, swap_sem, core_sem, row_sem, layer_sem, end_sem,
):
    row = lax.axis_index("row")
    me = lax.axis_index("layer")
    core = lax.rem(me, 2)
    half = other_raw.shape[1]
    width = fit.shape[0]
    weights, block_rows, points = turned_ref.shape
    pairs = own_turned.shape[0]
    entries = owner_ref.shape[1]
    half_owned = owned // 2
    slices = peers * owned
    group = 8 if entries % 8 == 0 else 1
    owner_width = half // 2
    mate = row + 1 - 2 * lax.rem(row, 2)
    cross = lax.rem(row + 2, peers)
    opposite = peers - 1 - row
    is_end = jnp.logical_or(row == 0, row == peers - 1)
    is_middle = jnp.logical_not(is_end)
    layer_peers = [lax.rem(me + k, 4) for k in range(1, 4)]
    partner = layer_peers[1]
    sibling = me + 1 - 2 * core
    order = (opposite, cross, mate, row)

    first_own = pl.multiple_of(me // 2 * half, half)
    first_other = pl.multiple_of((1 - me // 2) * half, half)
    other_copy = pltpu.make_async_copy(layers_ref.at[:, pl.ds(first_other, half)], other_raw, in_sem.at[0])
    own_copy = pltpu.make_async_copy(layers_ref.at[:, pl.ds(first_own, half)], own_raw, in_sem.at[1])
    fit_copy = pltpu.make_async_copy(fitting_ref, fit, in_sem.at[2])
    other_copy.start()
    own_copy.start()

    barrier = pltpu.get_barrier_semaphore()
    for peer in (mate, cross, opposite):
        pl.semaphore_signal(barrier, inc=1, device_id={"row": peer}, device_id_type=MESH)
    for peer in layer_peers:
        pl.semaphore_signal(barrier, inc=1, device_id={"layer": peer}, device_id_type=MESH)

    index_table(
        owner_ref[...], local_ref[...], block_ref[...], weight_ref[...], owned, weights, slices, meta
    )

    def remote(source, target, sems, where, axis, peer):
        return pltpu.make_async_remote_copy(
            src_ref=source,
            dst_ref=target,
            send_sem=sems.at[(0, *where)],
            recv_sem=sems.at[(1, *where)],
            device_id={axis: peer},
            device_id_type=MESH,
        )

    def turn(raw, targets):
        def body(pair, carry):
            turned = raw[pl.ds(pl.multiple_of(pair * points, points), points), :].T
            for (low, high), (target, base) in zip(spans, targets):
                size = high - low
                for side in range(2):
                    start = side * owner_width + low
                    target[pair, base + side * size : base + (side + 1) * size, :] = turned[
                        start : start + size
                    ]
            return carry

        lax.fori_loop(0, pairs, body, 0, unroll=4)

    other_copy.wait()
    turn(other_raw, [(refs["swap_out"], 0) for refs in chunk_refs])
    pl.semaphore_wait(barrier, peers - 1 + 3)
    meta_copy = remote(meta, got_index, meta_sem, (0,), "layer", partner)
    meta_copy.start()
    swaps = [
        remote(refs["swap_out"], refs["swap_in"], swap_sem, (index,), "layer", partner)
        for index, refs in enumerate(chunk_refs)
    ]
    for copy in swaps:
        copy.start()
    index_copy = pltpu.make_async_copy(meta, own_index, meta_sem.at[2, 0])
    index_copy.start()
    fit_copy.start()

    wide_table[...] = jnp.zeros_like(wide_table)
    for index in range(weights):
        wide_table[index, 0:block_rows, :] = turned_ref[index]
        wide_table[weights + index, block_rows:, :] = turned_ref[index]
    own_sums[0] = jnp.zeros(own_sums.shape[1:], own_sums.dtype)
    got_sums[0] = jnp.zeros(got_sums.shape[1:], got_sums.dtype)
    own_copy.wait()
    turn(own_raw, [(own_turned, 2 * low) for low, _ in spans])
    index_copy.wait()

    def sum_terms(index_ref, rows_ref, sums_ref, size):
        def body(step, carry):
            terms = []
            for offset in range(group):
                entry = step * group + offset
                terms.append(
                    jnp.dot(
                        rows_ref[index_ref[0, entry]],
                        wide_table[index_ref[1, entry]],
                        preferred_element_type=jnp.float32,
                    )
                )
            running = sums_ref[step * group, 0:size, :]
            for offset in range(group):
                entry = step * group + offset
                running = terms[offset] + index_ref[2, entry].astype(jnp.float32) * running
                sums_ref[entry + 1, 0:size, :] = running
            return carry

        lax.fori_loop(0, entries // group, body, 0)

    sum_terms(own_index, own_turned, own_sums, half)
    meta_copy.wait_recv()

    def core_copy(chunk, place):
        refs = chunk_refs[chunk]
        return remote(
            refs["core_out"].at[place], refs["core_in"].at[place], core_sem, (chunk, place), "layer", sibling
        )

    def row_copy(chunk, slot, source, peer):
        refs = chunk_refs[chunk]
        return remote(
            refs["row_out"].at[source], refs["row_in"].at[slot], row_sem, (chunk, slot), "row", peer
        )

    def layer_copy(chunk, k):
        refs = chunk_refs[chunk]
        return remote(
            refs["pieces"].at[me], refs["pieces"].at[me], layer_sem, (chunk, k), "layer", layer_peers[k]
        )

    def end_copy(chunk, slot, source, peer):
        refs = chunk_refs[chunk]
        return remote(
            refs["product"].at[source], refs["landed"].at[slot], end_sem, (chunk, slot), "row", peer
        )

    def partial(chunk, owner, which, index):
        low, high = spans[chunk]
        name = owner * owned + which * half_owned + index
        return (
            own_sums[own_index[3, name], 2 * low : 2 * high, :]
            + got_sums[got_index[3, name], 0 : 2 * (high - low), :]
        )

    def begin(chunk):
        refs = chunk_refs[chunk]
        low, high = spans[chunk]
        swaps[chunk].wait_recv()
        sum_terms(got_index, refs["swap_in"], got_sums, 2 * (high - low))

    def share(chunk):
        refs = chunk_refs[chunk]
        for place, owner in enumerate(order):

            def body(index, carry):
                refs["core_out"][place, index] = partial(chunk, owner, 1 - core, index).astype(jnp.bfloat16)
                return carry

            lax.fori_loop(0, half_owned, body, 0, unroll=4)
            core_copy(chunk, place).start()

    def spread(chunk):
        refs = chunk_refs[chunk]
        low, high = spans[chunk]
        for place, owner in enumerate(order):
            core_copy(chunk, place).wait_recv()

            def body(index, carry):
                value = partial(chunk, owner, core, index) + refs["core_in"][place, index].astype(jnp.float32)
                if place < 3:
                    refs["row_out"][place, index] = value.astype(jnp.bfloat16)
                else:
                    own_part[index, 2 * low : 2 * high, :] = value
                return carry

            lax.fori_loop(0, half_owned, body, 0, unroll=4)
            if place == 0:

                @pl.when(is_end)
                def _():
                    row_copy(chunk, 3, 0, mate).start()

                @pl.when(is_middle)
                def _():
                    row_copy(chunk, 2, 0, opposite).start()

            elif place == 1:

                @pl.when(is_end)
                def _():
                    row_copy(chunk, 1, 1, cross).start()

            elif place == 2:
                row_copy(chunk, 0, 2, mate).start()

    def join(chunk):
        refs = chunk_refs[chunk]

        @pl.when(is_middle)
        def _():
            row_copy(chunk, 3, 0, mate).wait_recv()
            refs["row_out"][1] = (
                refs["row_out"][1].astype(jnp.float32) + refs["row_in"][3].astype(jnp.float32)
            ).astype(jnp.bfloat16)
            row_copy(chunk, 1, 1, cross).start()

    def settle(chunk):
        refs = chunk_refs[chunk]
        low, high = spans[chunk]
        row_copy(chunk, 0, 2, mate).wait_recv()
        row_copy(chunk, 1, 1, cross).wait_recv()

        def store(slots):
            value = own_part[:, 2 * low : 2 * high, :]
            for slot in range(slots):
                value = value + refs["row_in"][slot].astype(jnp.float32)
            refs["pieces"][me] = value.astype(jnp.bfloat16)

        @pl.when(is_end)
        def _():
            store(2)

        @pl.when(is_middle)
        def _():
            row_copy(chunk, 2, 0, opposite).wait_recv()
            store(3)

        for k in (1, 0, 2):
            layer_copy(chunk, k).start()

    def multiply(chunk):
        refs = chunk_refs[chunk]
        low, high = spans[chunk]
        size = 2 * (high - low)
        for k in range(3):
            layer_copy(chunk, k).wait_recv()
        for piece in range(4):
            side, which = piece // 2, piece % 2
            for index in range(half_owned):
                first = (which * half_owned + index) * points
                left[side * size : (side + 1) * size, first : first + points] = refs["pieces"][piece, index]
        for start in range(0, width, 256):
            stop = min(start + 256, width)
            total[4 * low : 4 * high, start:stop] = lax.dot_general(
                left[0 : 2 * size, :],
                fit[start:stop, :],
                (((1,), (1,)), ((), ())),
                preferred_element_type=jnp.float32,
            )

    def total_of(chunk, owner):
        low, high = spans[chunk]
        size = high - low
        return total[pl.ds(pl.multiple_of(4 * low + owner * size, size), size), 0:width]

    def deliver(chunk):
        refs = chunk_refs[chunk]
        padded = refs["product"].shape[2]
        if width < padded:
            shape = (3, refs["product"].shape[1], 128)
            refs["product"][:, :, padded - 128 :] = jnp.zeros(shape, jnp.bfloat16)

        def fill(place):
            refs["product"][place, :, 0:width] = total_of(chunk, order[place]).astype(jnp.bfloat16)

        @pl.when(is_end)
        def _():
            fill(0)
            end_copy(chunk, 3, 0, mate).start()
            fill(1)
            end_copy(chunk, 1, 1, cross).start()
            fill(2)
            end_copy(chunk, 0, 2, mate).start()

        @pl.when(is_middle)
        def _():
            fill(0)
            end_copy(chunk, 2, 0, opposite).start()
            fill(2)
            end_copy(chunk, 0, 2, mate).start()

    def pass_on(chunk):
        refs = chunk_refs[chunk]

        @pl.when(is_middle)
        def _():
            end_copy(chunk, 3, 0, mate).wait_recv()
            refs["product"][1, :, 0:width] = (
                total_of(chunk, cross) + refs["landed"][3, :, 0:width].astype(jnp.float32)
            ).astype(jnp.bfloat16)
            end_copy(chunk, 1, 1, cross).start()

    def finish(chunk):
        refs = chunk_refs[chunk]
        low, high = spans[chunk]
        end_copy(chunk, 0, 2, mate).wait_recv()
        end_copy(chunk, 1, 1, cross).wait_recv()

        def store(slots):
            value = total_of(chunk, row)
            for slot in range(slots):
                value = value + refs["landed"][slot, :, 0:width].astype(jnp.float32)
            out_ref[low:high, :] = value.astype(out_ref.dtype)

        @pl.when(is_end)
        def _():
            store(2)

        @pl.when(is_middle)
        def _():
            end_copy(chunk, 2, 0, opposite).wait_recv()
            store(3)

    chunks = len(spans)
    for chunk in range(chunks):
        begin(chunk)
        if chunk > 0:
            join(chunk - 1)
        share(chunk)
        spread(chunk)
        if chunk > 0:
            settle(chunk - 1)
        if chunk == 1:
            fit_copy.wait()
        if chunk > 1:
            multiply(chunk - 2)
            deliver(chunk - 2)
    join(chunks - 1)
    if chunks == 1:
        fit_copy.wait()
    if chunks > 1:
        multiply(chunks - 2)
        deliver(chunks - 2)
    settle(chunks - 1)
    for chunk in range(chunks - 1):
        pass_on(chunk)
    multiply(chunks - 1)
    deliver(chunks - 1)
    for chunk in range(chunks - 1):
        finish(chunk)
    pass_on(chunks - 1)
    finish(chunks - 1)

    meta_copy.wait_send()
    for copy in swaps:
        copy.wait_send()
    for chunk in range(chunks):
        for place in range(4):
            core_copy(chunk, place).wait_send()
        for k in range(3):
            layer_copy(chunk, k).wait_send()
        for copy_of in (row_copy, end_copy):
            copy_of(chunk, 0, 2, mate).wait_send()
            copy_of(chunk, 1, 1, cross).wait_send()

            @pl.when(is_end)
            def _():
                copy_of(chunk, 3, 0, mate).wait_send()

            @pl.when(is_middle)
            def _():
                copy_of(chunk, 2, 0, opposite).wait_send()


def local_fused(layers, table, fitting, owner, local_slice, block_index, weight_index):
    rows_dev, columns = layers.shape[1:]
    weights, points, block_rows = table.shape
    entries = owner.shape[1]
    peers = lax.axis_size("row")
    depth, width = fitting.shape
    owned = depth // points
    half = columns // 2
    out_rows = columns // peers
    padded = -(-width // 128) * 128
    pairs = rows_dev // points
    cuts = cuts_of(out_rows)
    spans = list(zip(cuts[:-1], cuts[1:]))
    bf16, f32 = jnp.bfloat16, jnp.float32
    dma = pltpu.SemaphoreType.DMA

    def chunk_scratch(low, high):
        size = high - low
        cols = 2 * size
        return {
            "swap_out": pltpu.VMEM((pairs, cols, points), bf16),
            "swap_in": pltpu.VMEM((pairs, cols, points), bf16),
            "core_out": pltpu.VMEM((4, owned // 2, cols, points), bf16),
            "core_in": pltpu.VMEM((4, owned // 2, cols, points), bf16),
            "row_out": pltpu.VMEM((3, owned // 2, cols, points), bf16),
            "row_in": pltpu.VMEM((4, owned // 2, cols, points), bf16),
            "pieces": pltpu.VMEM((4, owned // 2, cols, points), bf16),
            "product": pltpu.VMEM((3, size, padded), bf16),
            "landed": pltpu.VMEM((4, size, padded), bf16),
        }

    widest = 2 * max(high - low for low, high in spans)
    count = len(spans)
    vmem = pl.BlockSpec(memory_space=pltpu.VMEM)
    any_space = pl.BlockSpec(memory_space=pl.ANY)
    return pl.pallas_call(
        functools.partial(fused_kernel, peers, owned, spans),
        out_shape=jax.ShapeDtypeStruct((out_rows, width), bf16),
        in_specs=[any_space, vmem, vmem, vmem, vmem, vmem, any_space],
        out_specs=vmem,
        scratch_shapes=[
            pltpu.VMEM((rows_dev, half), bf16),
            pltpu.VMEM((rows_dev, half), bf16),
            pltpu.VMEM((pairs, half, points), bf16),
            pltpu.VMEM((2 * weights, points, points), bf16),
            pltpu.VMEM((entries + 1, half, points), f32),
            pltpu.VMEM((entries + 1, widest, points), f32),
            pltpu.VMEM((8, 128), jnp.int32),
            pltpu.SMEM((8, 128), jnp.int32),
            pltpu.SMEM((8, 128), jnp.int32),
            pltpu.VMEM((width, depth), bf16),
            pltpu.VMEM((2 * widest, depth), bf16),
            pltpu.VMEM((columns, padded), f32),
            pltpu.VMEM((owned // 2, half, points), f32),
            [chunk_scratch(low, high) for low, high in spans],
            dma((3,)),
            dma((3, 1)),
            dma((2, count)),
            dma((2, count, 4)),
            dma((2, count, 4)),
            dma((2, count, 3)),
            dma((2, count, 4)),
        ],
        compiler_params=pltpu.CompilerParams(collective_id=0, has_side_effects=True),
    )(
        layers[0],
        table.transpose(0, 2, 1),
        owner[:, :, 0],
        local_slice,
        block_index,
        weight_index,
        fitting.T,
    )


def cuts_of(out_rows):
    quarter = out_rows // 4
    return [0, quarter, 2 * quarter, out_rows]


def local(layers, table, fitting, owner, local_slice, block_index, weight_index):
    arguments = (layers, table, fitting, owner, local_slice, block_index, weight_index)
    entries, peers, group = owner.shape[1], lax.axis_size("row"), lax.axis_size("layer")
    _, points, block_rows = table.shape
    raw_rows = max(2, 2 * entries // peers) * block_rows
    reduced_rows = fitting.shape[0] // group
    slices = peers * fitting.shape[0] // points
    fits = points == 128 and block_rows == 64 and layers.shape[2] == 256
    fits = fits and entries <= 128 and slices <= 128
    if group == 4 and peers == 4 and raw_rows > reduced_rows and fits:
        return local_fused(*arguments)
    return local_rows(*arguments)


def solution(mesh):
    return jax.shard_map(
        local,
        mesh=mesh,
        in_specs=(
            P("layer", "row", "panel"),
            P(),
            P("row", "layer"),
            P("layer", "row", None),
            P("layer", "row"),
            P("layer", "row"),
            P("layer", "row"),
        ),
        out_specs=P(("panel", "row"), "layer"),
        check_vma=False,
    )
```

time: 74.3 us -> 57.9 us (0.78)
  Pallas kernels: 71.1 us -> 56 us
  other arithmetic: 1.29 us -> 0 us
    pallas_call x3 -> x1, Pallas kernels: 71.1 us -> 56 us  [local_fused(): pl.pallas_call(functools.partial(fused_kernel, peers, owned, spans), out_...]
    another operation x1 -> x0, other arithmetic: 1.29 us -> none  [local_reduced(): jnp.stack([owner[0, :, 0], local_slice[0], block_index[0], weight_index[0]])]
where the time goes in v1:
time: 57.9 us; the launch traced here: 57.7 us
  Pallas kernels  56 us (97%)
  local copies, waits for them, and re-layouts  1.63 us (3%)
    pallas_call x1, Pallas kernels, local_fused(): pl.pallas_call(functools.partial(fused_kernel, peers, owned, spans), out_...  56 us
    unnamed x1, local copies, waits for them, and re-layouts  1.63 us

profile of v1, /device:TPU:0, one launch (start us, length us, event | category | flops | bytes accessed | tf_op | source)
XLA Modules:
  0.0 57.7 jit_solution(11049165289886630008)
XLA Ops:
  0.0 56.0 %shard_map.73 = bf16[64,1650]{1,0:T(8,128)(2,1)} custom-call(bf16[2048,256]{1,0:T(8,128)(2,1)} %bitcast.5, bf16[16,64,128]{2,1,0:T(8,128)(2,1)} %bitcast.6, s32[1,32]{1,0:T(1,128)} %bitcast.7, s32[1,32]{1,0:T(1,128)} %local_ref.1, s32[1,32]{1,0:T(1,128)} %block_ref.1, s32[1,32]{1,0:T(1,128)} %weight_ref.1, bf16[1650,2048]{1,0:T(8,128)(2,1)} %bitcast.4), custom_call_target="tpu_custom_call" | custom-call | tf_op jit(solution)/shard_map/pallas_call | solution.py:504
  56.0 1.6 %copy.9 = bf16[64,1650]{1,0:T(8,128)(2,1)} copy(bf16[64,1650]{1,0:T(8,128)(2,1)} %shard_map.73) | data formatting | bytes 422400

commit v2 on v1

v2 whole, which is shorter than its diff:
```python
import functools

import jax
import jax.numpy as jnp
from jax import lax
from jax.experimental import pallas as pl
from jax.experimental.pallas import tpu as pltpu

MESH = pl.DeviceIdType.MESH
from jax.sharding import PartitionSpec as P


def local_rows(layers, table, fitting, owner, local_slice, block_index, weight_index):
    rows_dev = layers.shape[1]
    columns = layers.shape[2]
    slice_rows = table.shape[1]
    block_rows = table.shape[2]
    entries = owner.shape[1]
    peer_count = lax.axis_size("row")
    capacity = max(2, 2 * entries // peer_count)
    slot_count = peer_count * capacity
    owned_slices = fitting.shape[0] // slice_rows
    owner_now = owner[0, :, 0]
    local_now = local_slice[0]
    owner_match = (owner_now[:, None] == jnp.arange(peer_count, dtype=jnp.int32)[None, :]).astype(
        jnp.int32
    )
    slot_rank = jnp.sum((jnp.cumsum(owner_match, axis=0) - 1) * owner_match, axis=1)
    target = owner_now * capacity + slot_rank
    placed = target[None, :] == jnp.arange(slot_count, dtype=jnp.int32)[:, None]
    filled = jnp.any(placed, axis=1)
    source = jnp.sum(jnp.where(placed, jnp.arange(entries, dtype=jnp.int32)[None, :], 0), axis=1)
    send_local = jnp.where(filled, local_now[source], -1).reshape(peer_count, capacity)
    grouped = layers[0].reshape(rows_dev // block_rows, block_rows, columns)
    picked = grouped[block_index[0][source]].reshape(peer_count, capacity, block_rows, columns)
    send_weight = weight_index[0][source].reshape(peer_count, capacity)
    got_rows, got_weight, got_local = (
        lax.all_to_all(picked, "row", split_axis=0, concat_axis=0, tiled=True),
        lax.all_to_all(send_weight, "row", split_axis=0, concat_axis=0, tiled=True),
        lax.all_to_all(send_local, "row", split_axis=0, concat_axis=0, tiled=True),
    )
    pupil_terms = jnp.einsum(
        "ksb,kbc->ksc",
        table[got_weight.reshape(-1)],
        got_rows.reshape(slot_count, block_rows, columns),
        preferred_element_type=jnp.float32,
    ).astype(jnp.bfloat16)
    selector = (
        jnp.arange(owned_slices, dtype=jnp.int32)[:, None] == got_local.reshape(-1)[None, :]
    ).astype(jnp.bfloat16)
    partial_pupil = jnp.dot(
        selector,
        pupil_terms.reshape(slot_count, slice_rows * columns),
        preferred_element_type=jnp.float32,
    ).reshape(owned_slices * slice_rows, columns)
    pupil_rounded = lax.psum(partial_pupil, "layer").astype(jnp.bfloat16)
    return lax.psum_scatter(
        lax.dot_general(
            pupil_rounded, fitting, (((0,), (0,)), ((), ())), preferred_element_type=jnp.float32
        ),
        "row",
        scatter_dimension=0,
        tiled=True,
    ).astype(jnp.bfloat16)


def index_table(owner, local_slice, block, weight, owned, weights, slices, out_ref):
    entries = owner.shape[1]
    square = (entries, entries)
    down = lax.broadcasted_iota(jnp.int32, square, 0)
    along = lax.broadcasted_iota(jnp.int32, square, 1)

    def upright(row):
        return jnp.sum(jnp.where(down == along, jnp.broadcast_to(row, square), 0), axis=1, keepdims=True)

    place = owner * owned + local_slice
    place_up = upright(place)
    place_row = jnp.broadcast_to(place, square)
    twin = (place_row == place_up) & (along < down)
    rank = jnp.sum(((place_row < place_up) | twin).astype(jnp.int32), axis=1, keepdims=True)
    follows = (jnp.sum(twin.astype(jnp.int32), axis=1, keepdims=True) > 0).astype(jnp.int32)
    code = upright(block * weights + weight)
    moved = rank == along
    code = jnp.sum(jnp.where(moved, jnp.broadcast_to(code, square), 0), axis=0, keepdims=True)
    follows = jnp.sum(jnp.where(moved, jnp.broadcast_to(follows, square), 0), axis=0, keepdims=True)
    names = lax.broadcasted_iota(jnp.int32, (entries, slices), 1)
    place_wide = jnp.broadcast_to(place_up, (entries, slices))
    until = jnp.sum((place_wide <= names).astype(jnp.int32), axis=0, keepdims=True)
    held = jnp.sum((place_wide == names).astype(jnp.int32), axis=0, keepdims=True)
    block = code // weights
    out_ref[0:1, 0:entries] = block // 2
    out_ref[1:2, 0:entries] = (block % 2) * weights + code % weights
    out_ref[2:3, 0:entries] = follows
    out_ref[3:4, 0:slices] = jnp.where(held > 0, until, 0)


def fused_kernel(
    peers, owned, chunks, groups,
    layers_hbm, table_hbm, owner_hbm, local_hbm, block_hbm, weight_hbm, fitting_hbm, out_ref,
    other_raw, own_raw, turned_ref, owner_ref, local_ref, block_ref, weight_ref,
    own_turned, wide_table, own_sums, got_sums, meta, own_index, got_index,
    fit, left, total, own_part, chunk_refs, group_refs,
    in_sem, meta_sem, swap_sem, core_sem, row_sem, layer_sem, end_sem,
):
    row = lax.axis_index("row")
    me = lax.axis_index("layer")
    core = lax.rem(me, 2)
    side = me // 2
    half = other_raw.shape[1]
    width = fit.shape[0]
    weights, block_rows, points = turned_ref.shape
    pairs = own_turned.shape[0]
    entries = owner_ref.shape[1]
    half_owned = owned // 2
    slices = peers * owned
    step_entries = 8 if entries % 8 == 0 else 1
    owner_width = half // 2
    mate = row + 1 - 2 * lax.rem(row, 2)
    cross = lax.rem(row + 2, peers)
    opposite = peers - 1 - row
    is_end = jnp.logical_or(row == 0, row == peers - 1)
    is_middle = jnp.logical_not(is_end)
    layer_peers = [lax.rem(me + k, 4) for k in range(1, 4)]
    partner = layer_peers[1]
    sibling = me + 1 - 2 * core
    order = (opposite, cross, mate, row)
    swapped = range(1, len(chunks))

    first_own = pl.multiple_of(side * half, half)
    first_other = pl.multiple_of((1 - side) * half, half)
    small_copies = [
        pltpu.make_async_copy(source, target, in_sem.at[4 + index])
        for index, (source, target) in enumerate(
            (
                (owner_hbm, owner_ref),
                (local_hbm, local_ref),
                (block_hbm, block_ref),
                (weight_hbm, weight_ref),
            )
        )
    ]
    other_copy = pltpu.make_async_copy(layers_hbm.at[:, pl.ds(first_other, half)], other_raw, in_sem.at[0])
    own_copy = pltpu.make_async_copy(layers_hbm.at[:, pl.ds(first_own, half)], own_raw, in_sem.at[1])
    table_copy = pltpu.make_async_copy(table_hbm, turned_ref, in_sem.at[2])
    fit_copy = pltpu.make_async_copy(fitting_hbm, fit, in_sem.at[3])
    for copy in small_copies:
        copy.start()
    other_copy.start()
    own_copy.start()
    table_copy.start()

    barrier = pltpu.get_barrier_semaphore()
    for peer in (mate, cross, opposite):
        pl.semaphore_signal(barrier, inc=1, device_id={"row": peer}, device_id_type=MESH)
    for peer in layer_peers:
        pl.semaphore_signal(barrier, inc=1, device_id={"layer": peer}, device_id_type=MESH)

    def remote(source, target, sems, where, axis, peer):
        return pltpu.make_async_remote_copy(
            src_ref=source,
            dst_ref=target,
            send_sem=sems.at[(0, *where)],
            recv_sem=sems.at[(1, *where)],
            device_id={axis: peer},
            device_id_type=MESH,
        )

    def turn(raw, targets, early):
        low, high = chunks[0]["parts"][0][1:]
        early_rows = pl.ds(pl.multiple_of(early * (high - low), high - low), high - low)

        def body(pair, carry):
            turned = raw[pl.ds(pl.multiple_of(pair * points, points), points), :].T
            for chunk, target, base in targets:
                for part, start, stop in chunks[chunk]["parts"]:
                    first = part * owner_width + start
                    target[pair, base : base + stop - start, :] = turned[first : first + stop - start]
                    base += stop - start
            own_turned[pair, early_rows, :] = turned[low:high]
            return carry

        lax.fori_loop(0, pairs, body, 0, unroll=4)

    def sum_terms(index_ref, rows_ref, sums_ref, size):
        def body(step, carry):
            terms = []
            for offset in range(step_entries):
                entry = step * step_entries + offset
                terms.append(
                    jnp.dot(
                        rows_ref[index_ref[0, entry]],
                        wide_table[index_ref[1, entry]],
                        preferred_element_type=jnp.float32,
                    )
                )
            running = sums_ref[step * step_entries, 0:size, :]
            for offset in range(step_entries):
                entry = step * step_entries + offset
                running = terms[offset] + index_ref[2, entry].astype(jnp.float32) * running
                sums_ref[entry + 1, 0:size, :] = running
            return carry

        lax.fori_loop(0, entries // step_entries, body, 0)

    def core_copy(chunk, place):
        refs = chunk_refs[chunk]
        return remote(
            refs["core_out"].at[place], refs["core_in"].at[place], core_sem, (chunk, place), "layer", sibling
        )

    def row_copy(chunk, slot, source, peer):
        refs = chunk_refs[chunk]
        return remote(
            refs["row_out"].at[source], refs["row_in"].at[slot], row_sem, (chunk, slot), "row", peer
        )

    def layer_copy(chunk, k):
        refs = chunk_refs[chunk]
        return remote(
            refs["pieces"].at[me], refs["pieces"].at[me], layer_sem, (chunk, k), "layer", layer_peers[k]
        )

    def end_copy(number, slot, source, peer):
        refs = group_refs[number]
        return remote(
            refs["product"].at[source], refs["landed"].at[slot], end_sem, (number, slot), "row", peer
        )

    def rows_of(chunk):
        base = chunks[chunk]["base"]
        return slice(base, base + chunks[chunk]["columns"])

    def partial(chunk, owner, which, index):
        name = owner * owned + which * half_owned + index
        value = own_sums[own_index[3, name], rows_of(chunk), :]
        if chunk > 0:
            value = value + got_sums[got_index[3, name], 0 : chunks[chunk]["columns"], :]
        return value

    def begin(chunk):
        swaps[chunk].wait_recv()
        sum_terms(got_index, chunk_refs[chunk]["swap_in"], got_sums, chunks[chunk]["columns"])

    def share(chunk):
        refs = chunk_refs[chunk]
        for place, owner in enumerate(order):

            def body(index, carry):
                refs["core_out"][place, index] = partial(chunk, owner, 1 - core, index).astype(jnp.bfloat16)
                return carry

            lax.fori_loop(0, half_owned, body, 0, unroll=4)
            core_copy(chunk, place).start()

    def spread(chunk):
        refs = chunk_refs[chunk]
        for place, owner in enumerate(order):
            core_copy(chunk, place).wait_recv()

            def body(index, carry):
                value = partial(chunk, owner, core, index) + refs["core_in"][place, index].astype(jnp.float32)
                if place < 3:
                    refs["row_out"][place, index] = value.astype(jnp.bfloat16)
                else:
                    own_part[index, rows_of(chunk), :] = value
                return carry

            lax.fori_loop(0, half_owned, body, 0, unroll=4)
            if place == 0:

                @pl.when(is_end)
                def _():
                    row_copy(chunk, 3, 0, mate).start()

                @pl.when(is_middle)
                def _():
                    row_copy(chunk, 2, 0, opposite).start()

            elif place == 1:

                @pl.when(is_end)
                def _():
                    row_copy(chunk, 1, 1, cross).start()

            elif place == 2:
                row_copy(chunk, 0, 2, mate).start()

    def join(chunk):
        refs = chunk_refs[chunk]

        @pl.when(is_middle)
        def _():
            row_copy(chunk, 3, 0, mate).wait_recv()
            refs["row_out"][1] = (
                refs["row_out"][1].astype(jnp.float32) + refs["row_in"][3].astype(jnp.float32)
            ).astype(jnp.bfloat16)
            row_copy(chunk, 1, 1, cross).start()

    def settle(chunk):
        refs = chunk_refs[chunk]
        row_copy(chunk, 0, 2, mate).wait_recv()
        row_copy(chunk, 1, 1, cross).wait_recv()

        def store(slots):
            value = own_part[:, rows_of(chunk), :]
            for slot in range(slots):
                value = value + refs["row_in"][slot].astype(jnp.float32)
            refs["pieces"][me] = value.astype(jnp.bfloat16)

        @pl.when(is_end)
        def _():
            store(2)

        @pl.when(is_middle)
        def _():
            row_copy(chunk, 2, 0, opposite).wait_recv()
            store(3)

        for k in (1, 0, 2):
            layer_copy(chunk, k).start()

    def multiply(number):
        low, high, members = groups[number]
        size = high - low
        for chunk in members:
            for k in range(3):
                layer_copy(chunk, k).wait_recv()
        for chunk in members:
            pieces = chunk_refs[chunk]["pieces"]
            for which in range(2):
                for index in range(half_owned):
                    first = (which * half_owned + index) * points
                    lanes = slice(first, first + points)
                    if chunk == 0:
                        value = pieces[which, index].astype(jnp.float32)
                        value = (value + pieces[2 + which, index].astype(jnp.float32)).astype(jnp.bfloat16)
                        left[0:size, lanes] = value[0:size]
                        left[2 * size : 3 * size, lanes] = value[size:]
                        continue
                    for far in range(2):
                        value = pieces[2 * far + which, index]
                        for place, (part, _, _) in enumerate(chunks[chunk]["parts"]):
                            target = (2 * far + part) * size
                            left[target : target + size, lanes] = value[place * size : (place + 1) * size]
        for start in range(0, width, 256):
            stop = min(start + 256, width)
            total[4 * low : 4 * high, start:stop] = lax.dot_general(
                left[0 : 4 * size, :],
                fit[start:stop, :],
                (((1,), (1,)), ((), ())),
                preferred_element_type=jnp.float32,
            )

    def total_of(number, owner):
        low, high, _ = groups[number]
        size = high - low
        return total[pl.ds(pl.multiple_of(4 * low + owner * size, size), size), 0:width]

    def deliver(number):
        product = group_refs[number]["product"]
        _, size, padded = product.shape
        if width < padded:
            product[:, :, padded - 128 :] = jnp.zeros((3, size, 128), jnp.bfloat16)

        def fill(place):
            product[place, :, 0:width] = total_of(number, order[place]).astype(jnp.bfloat16)

        @pl.when(is_end)
        def _():
            fill(0)
            end_copy(number, 3, 0, mate).start()
            fill(1)
            end_copy(number, 1, 1, cross).start()
            fill(2)
            end_copy(number, 0, 2, mate).start()

        @pl.when(is_middle)
        def _():
            fill(0)
            end_copy(number, 2, 0, opposite).start()
            fill(2)
            end_copy(number, 0, 2, mate).start()

    def pass_on(number):
        refs = group_refs[number]

        @pl.when(is_middle)
        def _():
            end_copy(number, 3, 0, mate).wait_recv()
            refs["product"][1, :, 0:width] = (
                total_of(number, cross) + refs["landed"][3, :, 0:width].astype(jnp.float32)
            ).astype(jnp.bfloat16)
            end_copy(number, 1, 1, cross).start()

    def finish(number):
        landed = group_refs[number]["landed"]
        low, high, _ = groups[number]
        end_copy(number, 0, 2, mate).wait_recv()
        end_copy(number, 1, 1, cross).wait_recv()

        def store(slots):
            value = total_of(number, row)
            for slot in range(slots):
                value = value + landed[slot, :, 0:width].astype(jnp.float32)
            out_ref[low:high, :] = value.astype(out_ref.dtype)

        @pl.when(is_end)
        def _():
            store(2)

        @pl.when(is_middle)
        def _():
            end_copy(number, 2, 0, opposite).wait_recv()
            store(3)

    for copy in small_copies:
        copy.wait()
    index_table(
        owner_ref[...], local_ref[...], block_ref[...], weight_ref[...], owned, weights, slices, meta
    )
    index_copy = pltpu.make_async_copy(meta, own_index, meta_sem.at[2, 0])
    index_copy.start()
    other_copy.wait()
    turn(other_raw, [(chunk, chunk_refs[chunk]["swap_out"], 0) for chunk in swapped], 1 - side)
    pl.semaphore_wait(barrier, peers - 1 + 3)
    meta_copy = remote(meta, got_index, meta_sem, (0,), "layer", partner)
    meta_copy.start()
    swaps = {
        chunk: remote(
            chunk_refs[chunk]["swap_out"], chunk_refs[chunk]["swap_in"], swap_sem, (chunk,), "layer", partner
        )
        for chunk in swapped
    }
    for copy in swaps.values():
        copy.start()
    fit_copy.start()
    own_copy.wait()
    turn(own_raw, [(chunk, own_turned, chunks[chunk]["base"]) for chunk in swapped], side)
    wide_table[...] = jnp.zeros_like(wide_table)
    table_copy.wait()
    for index in range(weights):
        wide_table[index, 0:block_rows, :] = turned_ref[index]
        wide_table[weights + index, block_rows:, :] = turned_ref[index]
    own_sums[0] = jnp.zeros(own_sums.shape[1:], own_sums.dtype)
    got_sums[0] = jnp.zeros(got_sums.shape[1:], got_sums.dtype)
    index_copy.wait()
    sum_terms(own_index, own_turned, own_sums, own_turned.shape[1])
    share(0)
    spread(0)
    meta_copy.wait_recv()
    begin(1)
    share(1)
    join(0)
    spread(1)
    begin(2)
    share(2)
    spread(2)
    join(1)
    settle(0)
    begin(3)
    share(3)
    spread(3)
    join(2)
    settle(1)
    begin(4)
    share(4)
    spread(4)
    join(3)
    settle(2)
    fit_copy.wait()
    multiply(0)
    join(4)
    deliver(0)
    settle(3)
    multiply(1)
    deliver(1)
    settle(4)
    pass_on(0)
    multiply(2)
    deliver(2)
    pass_on(1)
    multiply(3)
    deliver(3)
    pass_on(2)
    finish(0)
    finish(1)
    pass_on(3)
    finish(2)
    finish(3)

    meta_copy.wait_send()
    for copy in swaps.values():
        copy.wait_send()
    for chunk in range(len(chunks)):
        for place in range(4):
            core_copy(chunk, place).wait_send()
        for k in range(3):
            layer_copy(chunk, k).wait_send()

    def drain(copy_of, number):
        copy_of(number, 0, 2, mate).wait_send()
        copy_of(number, 1, 1, cross).wait_send()

        @pl.when(is_end)
        def _():
            copy_of(number, 3, 0, mate).wait_send()

        @pl.when(is_middle)
        def _():
            copy_of(number, 2, 0, opposite).wait_send()

    for chunk in range(len(chunks)):
        drain(row_copy, chunk)
    for number in range(len(groups)):
        drain(end_copy, number)


def plan_of(out_rows):
    cut = out_rows // 4
    marks = [cut * index for index in range(5)]
    spans = list(zip(marks[:-1], marks[1:]))
    low, high = spans[0]
    parts = [[(0, low, high)], [(1, low, high)]]
    parts += [[(0, start, stop), (1, start, stop)] for start, stop in spans[1:]]
    chunks, base = [], 0
    for number, part in enumerate(parts):
        columns = sum(stop - start for _, start, stop in part)
        if number == 0:
            columns = 2 * columns
        chunks.append({"parts": part, "columns": columns, "base": base})
        base += columns
    groups = [(low, high, (0, 1))]
    groups += [(start, stop, (number + 2,)) for number, (start, stop) in enumerate(spans[1:])]
    return chunks, groups, base


def local_fused(layers, table, fitting, owner, local_slice, block_index, weight_index):
    rows_dev, columns = layers.shape[1:]
    weights, points, block_rows = table.shape
    entries = owner.shape[1]
    peers = lax.axis_size("row")
    depth, width = fitting.shape
    owned = depth // points
    half = columns // 2
    out_rows = columns // peers
    padded = -(-width // 128) * 128
    pairs = rows_dev // points
    chunks, groups, held = plan_of(out_rows)
    bf16, f32 = jnp.bfloat16, jnp.float32
    dma = pltpu.SemaphoreType.DMA

    def chunk_scratch(number):
        cols = chunks[number]["columns"]
        slots = owned // 2
        refs = {
            "core_out": pltpu.VMEM((4, slots, cols, points), bf16),
            "core_in": pltpu.VMEM((4, slots, cols, points), bf16),
            "row_out": pltpu.VMEM((3, slots, cols, points), bf16),
            "row_in": pltpu.VMEM((4, slots, cols, points), bf16),
            "pieces": pltpu.VMEM((4, slots, cols, points), bf16),
        }
        if number > 0:
            refs["swap_out"] = pltpu.VMEM((pairs, cols, points), bf16)
            refs["swap_in"] = pltpu.VMEM((pairs, cols, points), bf16)
        return refs

    def group_scratch(number):
        low, high, _ = groups[number]
        return {
            "product": pltpu.VMEM((3, high - low, padded), bf16),
            "landed": pltpu.VMEM((4, high - low, padded), bf16),
        }

    widest = max(chunk["columns"] for chunk in chunks[1:])
    tallest = max(4 * (high - low) for low, high, _ in groups)
    vmem = pl.BlockSpec(memory_space=pltpu.VMEM)
    any_space = pl.BlockSpec(memory_space=pl.ANY)
    return pl.pallas_call(
        functools.partial(fused_kernel, peers, owned, chunks, groups),
        out_shape=jax.ShapeDtypeStruct((out_rows, width), bf16),
        in_specs=[any_space] * 7,
        out_specs=vmem,
        scratch_shapes=[
            pltpu.VMEM((rows_dev, half), bf16),
            pltpu.VMEM((rows_dev, half), bf16),
            pltpu.VMEM((weights, block_rows, points), bf16),
            pltpu.VMEM((1, entries), jnp.int32),
            pltpu.VMEM((1, entries), jnp.int32),
            pltpu.VMEM((1, entries), jnp.int32),
            pltpu.VMEM((1, entries), jnp.int32),
            pltpu.VMEM((pairs, held, points), bf16),
            pltpu.VMEM((2 * weights, points, points), bf16),
            pltpu.VMEM((entries + 1, held, points), f32),
            pltpu.VMEM((entries + 1, widest, points), f32),
            pltpu.VMEM((8, 128), jnp.int32),
            pltpu.SMEM((8, 128), jnp.int32),
            pltpu.SMEM((8, 128), jnp.int32),
            pltpu.VMEM((width, depth), bf16),
            pltpu.VMEM((tallest, depth), bf16),
            pltpu.VMEM((columns, padded), f32),
            pltpu.VMEM((owned // 2, held, points), f32),
            [chunk_scratch(number) for number in range(len(chunks))],
            [group_scratch(number) for number in range(len(groups))],
            dma((8,)),
            dma((3, 1)),
            dma((2, len(chunks))),
            dma((2, len(chunks), 4)),
            dma((2, len(chunks), 4)),
            dma((2, len(chunks), 3)),
            dma((2, len(groups), 4)),
        ],
        compiler_params=pltpu.CompilerParams(collective_id=0, has_side_effects=True),
    )(
        layers[0],
        table.transpose(0, 2, 1),
        owner[:, :, 0],
        local_slice,
        block_index,
        weight_index,
        fitting.T,
    )


def local(layers, table, fitting, owner, local_slice, block_index, weight_index):
    arguments = (layers, table, fitting, owner, local_slice, block_index, weight_index)
    entries, peers, group = owner.shape[1], lax.axis_size("row"), lax.axis_size("layer")
    _, points, block_rows = table.shape
    raw_rows = max(2, 2 * entries // peers) * block_rows
    reduced_rows = fitting.shape[0] // group
    slices = peers * fitting.shape[0] // points
    fits = points == 128 and block_rows == 64 and layers.shape[2] == 256
    fits = fits and entries <= 128 and slices <= 128
    if group == 4 and peers == 4 and raw_rows > reduced_rows and fits:
        return local_fused(*arguments)
    return local_rows(*arguments)


def solution(mesh):
    return jax.shard_map(
        local,
        mesh=mesh,
        in_specs=(
            P("layer", "row", "panel"),
            P(),
            P("row", "layer"),
            P("layer", "row", None),
            P("layer", "row"),
            P("layer", "row"),
            P("layer", "row"),
        ),
        out_specs=P(("panel", "row"), "layer"),
        check_vma=False,
    )
```

time: 57.9 us -> 50.3 us (0.87)
  Pallas kernels: 56 us -> 48.6 us
    pallas_call x1, Pallas kernels: 56 us -> 48.6 us  [local_fused(): pl.pallas_call(functools.partial(fused_kernel, peers, owned, chunks, grou...]
where the time goes in v2:
time: 50.3 us; the launch traced here: 50.2 us
  Pallas kernels  48.6 us (97%)
  local copies, waits for them, and re-layouts  1.63 us (3%)
    pallas_call x1, Pallas kernels, local_fused(): pl.pallas_call(functools.partial(fused_kernel, peers, owned, chunks, grou...  48.6 us
    unnamed x1, local copies, waits for them, and re-layouts  1.63 us

profile of v2, /device:TPU:0, one launch (start us, length us, event | category | flops | bytes accessed | tf_op | source)
XLA Modules:
  0.0 50.2 jit_solution(10320197583836755817)
XLA Ops:
  0.0 48.6 %shard_map.73 = bf16[64,1650]{1,0:T(8,128)(2,1)} custom-call(bf16[2048,256]{1,0:T(8,128)(2,1)} %bitcast.5, bf16[16,64,128]{2,1,0:T(8,128)(2,1)} %bitcast.6, s32[1,32]{1,0:T(1,128)} %bitcast.7, s32[1,32]{1,0:T(1,128)} %local_hbm.1, s32[1,32]{1,0:T(1,128)} %block_hbm.1, s32[1,32]{1,0:T(1,128)} %weight_hbm.1, bf16[1650,2048]{1,0:T(8,128)(2,1)} %bitcast.4), custom_call_target="tpu_custom_call" | custom-call | tf_op jit(solution)/shard_map/pallas_call | solution.py:578
  48.6 1.6 %copy.9 = bf16[64,1650]{1,0:T(8,128)(2,1)} copy(bf16[64,1650]{1,0:T(8,128)(2,1)} %shard_map.73) | data formatting | bytes 422400

commit v3 on v2

--- a/solution.py
+++ b/solution.py
@@ -96,10 +96,10 @@
 
 def fused_kernel(
     peers, owned, chunks, groups,
-    layers_hbm, table_hbm, owner_hbm, local_hbm, block_hbm, weight_hbm, fitting_hbm, out_ref,
+    layers_hbm, table_hbm, owner_hbm, local_hbm, block_hbm, weight_hbm, fitting_hbm, out_hbm,
     other_raw, own_raw, turned_ref, owner_ref, local_ref, block_ref, weight_ref,
     own_turned, wide_table, own_sums, got_sums, meta, own_index, got_index,
-    fit, left, total, own_part, chunk_refs, group_refs,
+    fit, left, total, own_part, result, chunk_refs, group_refs,
     in_sem, meta_sem, swap_sem, core_sem, row_sem, layer_sem, end_sem,
 ):
     row = lax.axis_index("row")
@@ -226,6 +226,12 @@
             refs["product"].at[source], refs["landed"].at[slot], end_sem, (number, slot), "row", peer
         )
 
+    def out_copy(number):
+        low, high, _ = groups[number]
+        return pltpu.make_async_copy(
+            result.at[low:high, :], out_hbm.at[low:high, :], in_sem.at[8 + number]
+        )
+
     def rows_of(chunk):
         base = chunks[chunk]["base"]
         return slice(base, base + chunks[chunk]["columns"])
@@ -266,21 +272,11 @@
                 return carry
 
             lax.fori_loop(0, half_owned, body, 0, unroll=4)
-            if place == 0:
+            if place < 2:
 
                 @pl.when(is_end)
                 def _():
-                    row_copy(chunk, 3, 0, mate).start()
-
-                @pl.when(is_middle)
-                def _():
-                    row_copy(chunk, 2, 0, opposite).start()
-
-            elif place == 1:
-
-                @pl.when(is_end)
-                def _():
-                    row_copy(chunk, 1, 1, cross).start()
+                    row_copy(chunk, 3 - place, place, mate).start()
 
             elif place == 2:
                 row_copy(chunk, 0, 2, mate).start()
@@ -288,33 +284,38 @@
     def join(chunk):
         refs = chunk_refs[chunk]
 
+        def merge(place, slot):
+            row_copy(chunk, slot, place, mate).wait_recv()
+            refs["row_out"][place] = (
+                refs["row_out"][place].astype(jnp.float32) + refs["row_in"][slot].astype(jnp.float32)
+            ).astype(jnp.bfloat16)
+
         @pl.when(is_middle)
         def _():
-            row_copy(chunk, 3, 0, mate).wait_recv()
-            refs["row_out"][1] = (
-                refs["row_out"][1].astype(jnp.float32) + refs["row_in"][3].astype(jnp.float32)
-            ).astype(jnp.bfloat16)
+            merge(1, 3)
             row_copy(chunk, 1, 1, cross).start()
+            merge(0, 2)
+            row_copy(chunk, 4, 0, opposite).start()
 
     def settle(chunk):
         refs = chunk_refs[chunk]
         row_copy(chunk, 0, 2, mate).wait_recv()
-        row_copy(chunk, 1, 1, cross).wait_recv()
-
-        def store(slots):
+
+        def store(slot):
             value = own_part[:, rows_of(chunk), :]
-            for slot in range(slots):
-                value = value + refs["row_in"][slot].astype(jnp.float32)
+            for part in (0, slot):
+                value = value + refs["row_in"][part].astype(jnp.float32)
             refs["pieces"][me] = value.astype(jnp.bfloat16)
 
         @pl.when(is_end)
         def _():
-            store(2)
+            row_copy(chunk, 1, 1, cross).wait_recv()
+            store(1)
 
         @pl.when(is_middle)
         def _():
-            row_copy(chunk, 2, 0, opposite).wait_recv()
-            store(3)
+            row_copy(chunk, 4, 0, opposite).wait_recv()
+            store(4)
 
         for k in (1, 0, 2):
             layer_copy(chunk, k).start()
@@ -367,51 +368,51 @@
 
         @pl.when(is_end)
         def _():
-            fill(0)
-            end_copy(number, 3, 0, mate).start()
-            fill(1)
-            end_copy(number, 1, 1, cross).start()
-            fill(2)
-            end_copy(number, 0, 2, mate).start()
-
-        @pl.when(is_middle)
-        def _():
-            fill(0)
-            end_copy(number, 2, 0, opposite).start()
-            fill(2)
-            end_copy(number, 0, 2, mate).start()
+            for place in range(2):
+                fill(place)
+                end_copy(number, 3 - place, place, mate).start()
+
+        fill(2)
+        end_copy(number, 0, 2, mate).start()
 
     def pass_on(number):
         refs = group_refs[number]
 
+        def merge(place, slot):
+            end_copy(number, slot, place, mate).wait_recv()
+            refs["product"][place, :, 0:width] = (
+                total_of(number, order[place]) + refs["landed"][slot, :, 0:width].astype(jnp.float32)
+            ).astype(jnp.bfloat16)
+
         @pl.when(is_middle)
         def _():
-            end_copy(number, 3, 0, mate).wait_recv()
-            refs["product"][1, :, 0:width] = (
-                total_of(number, cross) + refs["landed"][3, :, 0:width].astype(jnp.float32)
-            ).astype(jnp.bfloat16)
+            merge(1, 3)
             end_copy(number, 1, 1, cross).start()
+            merge(0, 2)
+            end_copy(number, 4, 0, opposite).start()
 
     def finish(number):
         landed = group_refs[number]["landed"]
         low, high, _ = groups[number]
         end_copy(number, 0, 2, mate).wait_recv()
-        end_copy(number, 1, 1, cross).wait_recv()
-
-        def store(slots):
+
+        def store(slot):
             value = total_of(number, row)
-            for slot in range(slots):
-                value = value + landed[slot, :, 0:width].astype(jnp.float32)
-            out_ref[low:high, :] = value.astype(out_ref.dtype)
+            for part in (0, slot):
+                value = value + landed[part, :, 0:width].astype(jnp.float32)
+            result[low:high, :] = value.astype(result.dtype)
 
         @pl.when(is_end)
         def _():
-            store(2)
+            end_copy(number, 1, 1, cross).wait_recv()
+            store(1)
 
         @pl.when(is_middle)
         def _():
-            end_copy(number, 2, 0, opposite).wait_recv()
-            store(3)
+            end_copy(number, 4, 0, opposite).wait_recv()
+            store(4)
+
+        out_copy(number).start()
 
     for copy in small_copies:
         copy.wait()
@@ -433,7 +434,6 @@
     }
     for copy in swaps.values():
         copy.start()
-    fit_copy.start()
     own_copy.wait()
     turn(own_raw, [(chunk, own_turned, chunks[chunk]["base"]) for chunk in swapped], side)
     wide_table[...] = jnp.zeros_like(wide_table)
@@ -452,19 +452,20 @@
     share(1)
     join(0)
     spread(1)
+    fit_copy.start()
     begin(2)
     share(2)
     spread(2)
     join(1)
-    settle(0)
     begin(3)
     share(3)
+    settle(0)
     spread(3)
     join(2)
-    settle(1)
     begin(4)
     share(4)
     spread(4)
+    settle(1)
     join(3)
     settle(2)
     fit_copy.wait()
@@ -499,20 +500,22 @@
 
     def drain(copy_of, number):
         copy_of(number, 0, 2, mate).wait_send()
-        copy_of(number, 1, 1, cross).wait_send()
 
         @pl.when(is_end)
         def _():
             copy_of(number, 3, 0, mate).wait_send()
+            copy_of(number, 2, 1, mate).wait_send()
 
         @pl.when(is_middle)
         def _():
-            copy_of(number, 2, 0, opposite).wait_send()
+            copy_of(number, 1, 1, cross).wait_send()
+            copy_of(number, 4, 0, opposite).wait_send()
 
     for chunk in range(len(chunks)):
         drain(row_copy, chunk)
     for number in range(len(groups)):
         drain(end_copy, number)
+        out_copy(number).wait()
 
 
 def plan_of(out_rows):
@@ -556,7 +559,7 @@
             "core_out": pltpu.VMEM((4, slots, cols, points), bf16),
             "core_in": pltpu.VMEM((4, slots, cols, points), bf16),
             "row_out": pltpu.VMEM((3, slots, cols, points), bf16),
-            "row_in": pltpu.VMEM((4, slots, cols, points), bf16),
+            "row_in": pltpu.VMEM((5, slots, cols, points), bf16),
             "pieces": pltpu.VMEM((4, slots, cols, points), bf16),
         }
         if number > 0:
@@ -568,18 +571,17 @@
         low, high, _ = groups[number]
         return {
             "product": pltpu.VMEM((3, high - low, padded), bf16),
-            "landed": pltpu.VMEM((4, high - low, padded), bf16),
+            "landed": pltpu.VMEM((5, high - low, padded), bf16),
         }
 
     widest = max(chunk["columns"] for chunk in chunks[1:])
     tallest = max(4 * (high - low) for low, high, _ in groups)
-    vmem = pl.BlockSpec(memory_space=pltpu.VMEM)
     any_space = pl.BlockSpec(memory_space=pl.ANY)
     return pl.pallas_call(
         functools.partial(fused_kernel, peers, owned, chunks, groups),
         out_shape=jax.ShapeDtypeStruct((out_rows, width), bf16),
         in_specs=[any_space] * 7,
-        out_specs=vmem,
+        out_specs=any_space,
         scratch_shapes=[
             pltpu.VMEM((rows_dev, half), bf16),
             pltpu.VMEM((rows_dev, half), bf16),
@@ -599,15 +601,16 @@
             pltpu.VMEM((tallest, depth), bf16),
             pltpu.VMEM((columns, padded), f32),
             pltpu.VMEM((owned // 2, held, points), f32),
+            pltpu.VMEM((out_rows, width), bf16),
             [chunk_scratch(number) for number in range(len(chunks))],
             [group_scratch(number) for number in range(len(groups))],
-            dma((8,)),
+            dma((8 + len(groups),)),
             dma((3, 1)),
             dma((2, len(chunks))),
             dma((2, len(chunks), 4)),
-            dma((2, len(chunks), 4)),
+            dma((2, len(chunks), 5)),
             dma((2, len(chunks), 3)),
-            dma((2, len(groups), 4)),
+            dma((2, len(groups), 5)),
         ],
         compiler_params=pltpu.CompilerParams(collective_id=0, has_side_effects=True),
     )(

time: 50.3 us -> 48.5 us (0.964)
  Pallas kernels: 48.6 us -> 46.7 us
    pallas_call x1, Pallas kernels: 48.6 us -> 46.7 us  [local_fused(): pl.pallas_call(functools.partial(fused_kernel, peers, owned, chunks, grou...]
where the time goes in v3:
time: 48.5 us; the launch traced here: 48.4 us
  Pallas kernels  46.7 us (96%)
  local copies, waits for them, and re-layouts  1.63 us (3%)
    pallas_call x1, Pallas kernels, local_fused(): pl.pallas_call(functools.partial(fused_kernel, peers, owned, chunks, grou...  46.7 us
    unnamed x1, local copies, waits for them, and re-layouts  1.63 us

profile of v3, /device:TPU:0, one launch (start us, length us, event | category | flops | bytes accessed | tf_op | source)
XLA Modules:
  0.0 48.4 jit_solution(7997479864616317839)
XLA Ops:
  0.0 46.7 %shard_map.73 = bf16[64,1650]{1,0:T(8,128)(2,1)} custom-call(bf16[2048,256]{1,0:T(8,128)(2,1)} %bitcast.5, bf16[16,64,128]{2,1,0:T(8,128)(2,1)} %bitcast.6, s32[1,32]{1,0:T(1,128)} %bitcast.7, s32[1,32]{1,0:T(1,128)} %local_hbm.1, s32[1,32]{1,0:T(1,128)} %block_hbm.1, s32[1,32]{1,0:T(1,128)} %weight_hbm.1, bf16[1650,2048]{1,0:T(8,128)(2,1)} %bitcast.4), custom_call_target="tpu_custom_call" | custom-call | tf_op jit(solution)/shard_map/pallas_call | solution.py:580
  46.7 1.6 %copy.9 = bf16[64,1650]{1,0:T(8,128)(2,1)} copy(bf16[64,1650]{1,0:T(8,128)(2,1)} %shard_map.73) | data formatting | bytes 422400

commit v4 on v3

--- a/solution.py
+++ b/solution.py
@@ -95,12 +95,12 @@
 
 
 def fused_kernel(
-    peers, owned, chunks, groups,
-    layers_hbm, table_hbm, owner_hbm, local_hbm, block_hbm, weight_hbm, fitting_hbm, out_hbm,
+    peers, owned, chunks, groups, units,
+    layers_hbm, table_hbm, owner_hbm, local_hbm, block_hbm, weight_hbm, fitting_hbm, result,
     other_raw, own_raw, turned_ref, owner_ref, local_ref, block_ref, weight_ref,
     own_turned, wide_table, own_sums, got_sums, meta, own_index, got_index,
-    fit, left, total, own_part, result, chunk_refs, group_refs,
-    in_sem, meta_sem, swap_sem, core_sem, row_sem, layer_sem, end_sem,
+    fit, left, total, own_part, chunk_refs, unit_refs,
+    in_sem, meta_sem, swap_sem, core_sem, row_send, row_recv, layer_send, layer_recv, end_send, end_recv,
 ):
     row = lax.axis_index("row")
     me = lax.axis_index("layer")
@@ -150,20 +150,23 @@
     table_copy.start()
 
     barrier = pltpu.get_barrier_semaphore()
-    for peer in (mate, cross, opposite):
+    for peer in (mate, 2 - row // 2):
         pl.semaphore_signal(barrier, inc=1, device_id={"row": peer}, device_id_type=MESH)
     for peer in layer_peers:
         pl.semaphore_signal(barrier, inc=1, device_id={"layer": peer}, device_id_type=MESH)
 
-    def remote(source, target, sems, where, axis, peer):
+    def remote(source, target, send, recv, axis, peer):
         return pltpu.make_async_remote_copy(
             src_ref=source,
             dst_ref=target,
-            send_sem=sems.at[(0, *where)],
-            recv_sem=sems.at[(1, *where)],
+            send_sem=send,
+            recv_sem=recv,
             device_id={axis: peer},
             device_id_type=MESH,
         )
+
+    def all_of(ref, sem):
+        return remote(ref, ref, sem, sem, "layer", partner)
 
     def turn(raw, targets, early):
         low, high = chunks[0]["parts"][0][1:]
@@ -181,56 +184,46 @@
 
         lax.fori_loop(0, pairs, body, 0, unroll=4)
 
-    def sum_terms(index_ref, rows_ref, sums_ref, size):
+    def sum_terms(index_ref, rows_ref, sums_ref, low, high):
         def body(step, carry):
             terms = []
             for offset in range(step_entries):
                 entry = step * step_entries + offset
                 terms.append(
                     jnp.dot(
-                        rows_ref[index_ref[0, entry]],
+                        rows_ref[index_ref[0, entry], low:high, :],
                         wide_table[index_ref[1, entry]],
                         preferred_element_type=jnp.float32,
                     )
                 )
-            running = sums_ref[step * step_entries, 0:size, :]
+            running = sums_ref[step * step_entries, low:high, :]
             for offset in range(step_entries):
                 entry = step * step_entries + offset
                 running = terms[offset] + index_ref[2, entry].astype(jnp.float32) * running
-                sums_ref[entry + 1, 0:size, :] = running
+                sums_ref[entry + 1, low:high, :] = running
             return carry
 
         lax.fori_loop(0, entries // step_entries, body, 0)
 
-    def core_copy(chunk, place):
+    def core_copy(chunk):
         refs = chunk_refs[chunk]
-        return remote(
-            refs["core_out"].at[place], refs["core_in"].at[place], core_sem, (chunk, place), "layer", sibling
-        )
+        sems = (core_sem.at[0, chunk], core_sem.at[1, chunk])
+        return remote(refs["core_out"], refs["core_in"], *sems, "layer", sibling)
 
     def row_copy(chunk, slot, source, peer):
         refs = chunk_refs[chunk]
-        return remote(
-            refs["row_out"].at[source], refs["row_in"].at[slot], row_sem, (chunk, slot), "row", peer
-        )
+        sems = (row_send.at[chunk], row_recv.at[chunk, max(slot, 1) - 1])
+        return remote(refs["row_out"].at[source], refs["row_in"].at[slot], *sems, "row", peer)
 
     def layer_copy(chunk, k):
-        refs = chunk_refs[chunk]
-        return remote(
-            refs["pieces"].at[me], refs["pieces"].at[me], layer_sem, (chunk, k), "layer", layer_peers[k]
-        )
-
-    def end_copy(number, slot, source, peer):
-        refs = group_refs[number]
-        return remote(
-            refs["product"].at[source], refs["landed"].at[slot], end_sem, (number, slot), "row", peer
-        )
-
-    def out_copy(number):
-        low, high, _ = groups[number]
-        return pltpu.make_async_copy(
-            result.at[low:high, :], out_hbm.at[low:high, :], in_sem.at[8 + number]
-        )
+        pieces = chunk_refs[chunk]["pieces"]
+        sems = (layer_send.at[chunk], layer_recv.at[chunk])
+        return remote(pieces.at[me], pieces.at[me], *sems, "layer", layer_peers[k])
+
+    def end_copy(unit, slot, source, peer):
+        refs = unit_refs[unit]
+        sems = (end_send.at[unit], end_recv.at[unit, max(slot, 1) - 1])
+        return remote(refs["product"].at[source], refs["landed"].at[slot], *sems, "row", peer)
 
     def rows_of(chunk):
         base = chunks[chunk]["base"]
@@ -245,7 +238,7 @@
 
     def begin(chunk):
         swaps[chunk].wait_recv()
-        sum_terms(got_index, chunk_refs[chunk]["swap_in"], got_sums, chunks[chunk]["columns"])
+        sum_terms(got_index, chunk_refs[chunk]["swap_in"], got_sums, 0, chunks[chunk]["columns"])
 
     def share(chunk):
         refs = chunk_refs[chunk]
@@ -256,12 +249,12 @@
                 return carry
 
             lax.fori_loop(0, half_owned, body, 0, unroll=4)
-            core_copy(chunk, place).start()
+        core_copy(chunk).start()
 
     def spread(chunk):
         refs = chunk_refs[chunk]
+        core_copy(chunk).wait_recv()
         for place, owner in enumerate(order):
-            core_copy(chunk, place).wait_recv()
 
             def body(index, carry):
                 value = partial(chunk, owner, core, index) + refs["core_in"][place, index].astype(jnp.float32)
@@ -276,58 +269,39 @@
 
                 @pl.when(is_end)
                 def _():
-                    row_copy(chunk, 3 - place, place, mate).start()
+                    row_copy(chunk, 2 + place, place, mate).start()
 
             elif place == 2:
                 row_copy(chunk, 0, 2, mate).start()
 
-    def join(chunk):
+    def join(chunk, place):
         refs = chunk_refs[chunk]
-
-        def merge(place, slot):
+        slot = 3 - place
+
+        @pl.when(is_middle)
+        def _():
             row_copy(chunk, slot, place, mate).wait_recv()
             refs["row_out"][place] = (
                 refs["row_out"][place].astype(jnp.float32) + refs["row_in"][slot].astype(jnp.float32)
             ).astype(jnp.bfloat16)
-
-        @pl.when(is_middle)
-        def _():
-            merge(1, 3)
-            row_copy(chunk, 1, 1, cross).start()
-            merge(0, 2)
-            row_copy(chunk, 4, 0, opposite).start()
+            row_copy(chunk, 1, place, order[place]).start()
 
     def settle(chunk):
         refs = chunk_refs[chunk]
-        row_copy(chunk, 0, 2, mate).wait_recv()
-
-        def store(slot):
-            value = own_part[:, rows_of(chunk), :]
-            for part in (0, slot):
-                value = value + refs["row_in"][part].astype(jnp.float32)
-            refs["pieces"][me] = value.astype(jnp.bfloat16)
-
-        @pl.when(is_end)
-        def _():
-            row_copy(chunk, 1, 1, cross).wait_recv()
-            store(1)
-
-        @pl.when(is_middle)
-        def _():
-            row_copy(chunk, 4, 0, opposite).wait_recv()
-            store(4)
-
+        all_of(refs["row_in"].at[0:2], row_recv.at[chunk, 0]).wait_recv()
+        value = own_part[:, rows_of(chunk), :]
+        for slot in range(2):
+            value = value + refs["row_in"][slot].astype(jnp.float32)
+        refs["pieces"][me] = value.astype(jnp.bfloat16)
         for k in (1, 0, 2):
             layer_copy(chunk, k).start()
 
-    def multiply(number):
+    def gather(number):
         low, high, members = groups[number]
         size = high - low
         for chunk in members:
-            for k in range(3):
-                layer_copy(chunk, k).wait_recv()
-        for chunk in members:
             pieces = chunk_refs[chunk]["pieces"]
+            all_of(pieces.at[0:3], layer_recv.at[chunk]).wait_recv()
             for which in range(2):
                 for index in range(half_owned):
                     first = (which * half_owned + index) * points
@@ -343,92 +317,89 @@
                         for place, (part, _, _) in enumerate(chunks[chunk]["parts"]):
                             target = (2 * far + part) * size
                             left[target : target + size, lanes] = value[place * size : (place + 1) * size]
-        for start in range(0, width, 256):
-            stop = min(start + 256, width)
+
+    def multiply(unit):
+        number, begins, ends = units[unit]
+        low, high, _ = groups[number]
+        for start in range(begins, ends, 256):
+            stop = min(start + 256, ends)
             total[4 * low : 4 * high, start:stop] = lax.dot_general(
-                left[0 : 4 * size, :],
+                left[0 : 4 * (high - low), :],
                 fit[start:stop, :],
                 (((1,), (1,)), ((), ())),
                 preferred_element_type=jnp.float32,
             )
 
-    def total_of(number, owner):
+    def total_of(unit, owner):
+        number, begins, ends = units[unit]
         low, high, _ = groups[number]
         size = high - low
-        return total[pl.ds(pl.multiple_of(4 * low + owner * size, size), size), 0:width]
-
-    def deliver(number):
-        product = group_refs[number]["product"]
+        return total[pl.ds(pl.multiple_of(4 * low + owner * size, size), size), begins:ends]
+
+    def deliver(unit):
+        product = unit_refs[unit]["product"]
+        _, begins, ends = units[unit]
         _, size, padded = product.shape
-        if width < padded:
+        if ends - begins < padded:
             product[:, :, padded - 128 :] = jnp.zeros((3, size, 128), jnp.bfloat16)
 
         def fill(place):
-            product[place, :, 0:width] = total_of(number, order[place]).astype(jnp.bfloat16)
+            product[place, :, 0 : ends - begins] = total_of(unit, order[place]).astype(jnp.bfloat16)
 
         @pl.when(is_end)
         def _():
             for place in range(2):
                 fill(place)
-                end_copy(number, 3 - place, place, mate).start()
+                end_copy(unit, 2 + place, place, mate).start()
 
         fill(2)
-        end_copy(number, 0, 2, mate).start()
-
-    def pass_on(number):
-        refs = group_refs[number]
-
-        def merge(place, slot):
-            end_copy(number, slot, place, mate).wait_recv()
-            refs["product"][place, :, 0:width] = (
-                total_of(number, order[place]) + refs["landed"][slot, :, 0:width].astype(jnp.float32)
-            ).astype(jnp.bfloat16)
+        end_copy(unit, 0, 2, mate).start()
+
+    def pass_on(unit):
+        product, landed = unit_refs[unit]["product"], unit_refs[unit]["landed"]
+        _, begins, ends = units[unit]
+        lanes = slice(0, ends - begins)
 
         @pl.when(is_middle)
         def _():
-            merge(1, 3)
-            end_copy(number, 1, 1, cross).start()
-            merge(0, 2)
-            end_copy(number, 4, 0, opposite).start()
-
-    def finish(number):
-        landed = group_refs[number]["landed"]
+            for place in (1, 0):
+                slot = 3 - place
+                end_copy(unit, slot, place, mate).wait_recv()
+                product[place, :, lanes] = (
+                    total_of(unit, order[place]) + landed[slot, :, lanes].astype(jnp.float32)
+                ).astype(jnp.bfloat16)
+                end_copy(unit, 1, place, order[place]).start()
+
+    def finish(unit):
+        landed = unit_refs[unit]["landed"]
+        number, begins, ends = units[unit]
         low, high, _ = groups[number]
-        end_copy(number, 0, 2, mate).wait_recv()
-
-        def store(slot):
-            value = total_of(number, row)
-            for part in (0, slot):
-                value = value + landed[part, :, 0:width].astype(jnp.float32)
-            result[low:high, :] = value.astype(result.dtype)
-
-        @pl.when(is_end)
-        def _():
-            end_copy(number, 1, 1, cross).wait_recv()
-            store(1)
-
-        @pl.when(is_middle)
-        def _():
-            end_copy(number, 4, 0, opposite).wait_recv()
-            store(4)
-
-        out_copy(number).start()
+        all_of(landed.at[0:2], end_recv.at[unit, 0]).wait_recv()
+        value = total_of(unit, row)
+        for slot in range(2):
+            value = value + landed[slot, :, 0 : ends - begins].astype(jnp.float32)
+        result[low:high, begins:ends] = value.astype(result.dtype)
 
     for copy in small_copies:
         copy.wait()
     index_table(
         owner_ref[...], local_ref[...], block_ref[...], weight_ref[...], owned, weights, slices, meta
     )
-    index_copy = pltpu.make_async_copy(meta, own_index, meta_sem.at[2, 0])
+    index_copy = pltpu.make_async_copy(meta, own_index, meta_sem.at[2])
     index_copy.start()
     other_copy.wait()
     turn(other_raw, [(chunk, chunk_refs[chunk]["swap_out"], 0) for chunk in swapped], 1 - side)
-    pl.semaphore_wait(barrier, peers - 1 + 3)
-    meta_copy = remote(meta, got_index, meta_sem, (0,), "layer", partner)
+    pl.semaphore_wait(barrier, 4 + 2 * lax.rem((row + 1) // 2, 2))
+    meta_copy = remote(meta, got_index, meta_sem.at[0], meta_sem.at[1], "layer", partner)
     meta_copy.start()
     swaps = {
         chunk: remote(
-            chunk_refs[chunk]["swap_out"], chunk_refs[chunk]["swap_in"], swap_sem, (chunk,), "layer", partner
+            chunk_refs[chunk]["swap_out"],
+            chunk_refs[chunk]["swap_in"],
+            swap_sem.at[0, chunk - 1],
+            swap_sem.at[1, chunk - 1],
+            "layer",
+            partner,
         )
         for chunk in swapped
     }
@@ -444,81 +415,78 @@
     own_sums[0] = jnp.zeros(own_sums.shape[1:], own_sums.dtype)
     got_sums[0] = jnp.zeros(got_sums.shape[1:], got_sums.dtype)
     index_copy.wait()
-    sum_terms(own_index, own_turned, own_sums, own_turned.shape[1])
+    early_rows = chunks[0]["columns"]
+    sum_terms(own_index, own_turned, own_sums, 0, early_rows)
     share(0)
     spread(0)
+    sum_terms(own_index, own_turned, own_sums, early_rows, own_turned.shape[1])
     meta_copy.wait_recv()
     begin(1)
     share(1)
-    join(0)
+    join(0, 1)
     spread(1)
+    join(0, 0)
     fit_copy.start()
     begin(2)
     share(2)
+    join(1, 1)
     spread(2)
-    join(1)
+    join(1, 0)
     begin(3)
     share(3)
     settle(0)
     spread(3)
-    join(2)
+    join(2, 1)
+    settle(1)
     begin(4)
     share(4)
+    join(2, 0)
     spread(4)
-    settle(1)
-    join(3)
+    join(3, 1)
     settle(2)
     fit_copy.wait()
+    gather(0)
     multiply(0)
-    join(4)
+    join(3, 0)
     deliver(0)
+    join(4, 1)
+    join(4, 0)
     settle(3)
+    gather(1)
     multiply(1)
     deliver(1)
     settle(4)
     pass_on(0)
+    gather(2)
     multiply(2)
     deliver(2)
     pass_on(1)
+    gather(3)
     multiply(3)
     deliver(3)
+    multiply(4)
+    deliver(4)
     pass_on(2)
     finish(0)
     finish(1)
     pass_on(3)
+    pass_on(4)
     finish(2)
     finish(3)
+    finish(4)
 
     meta_copy.wait_send()
     for copy in swaps.values():
         copy.wait_send()
-    for chunk in range(len(chunks)):
-        for place in range(4):
-            core_copy(chunk, place).wait_send()
-        for k in range(3):
-            layer_copy(chunk, k).wait_send()
-
-    def drain(copy_of, number):
-        copy_of(number, 0, 2, mate).wait_send()
-
-        @pl.when(is_end)
-        def _():
-            copy_of(number, 3, 0, mate).wait_send()
-            copy_of(number, 2, 1, mate).wait_send()
-
-        @pl.when(is_middle)
-        def _():
-            copy_of(number, 1, 1, cross).wait_send()
-            copy_of(number, 4, 0, opposite).wait_send()
-
-    for chunk in range(len(chunks)):
-        drain(row_copy, chunk)
-    for number in range(len(groups)):
-        drain(end_copy, number)
-        out_copy(number).wait()
-
-
-def plan_of(out_rows):
+    for chunk, refs in enumerate(chunk_refs):
+        core_copy(chunk).wait_send()
+        all_of(refs["row_out"], row_send.at[chunk]).wait_send()
+        all_of(refs["pieces"].at[0:3], layer_send.at[chunk]).wait_send()
+    for unit, refs in enumerate(unit_refs):
+        all_of(refs["product"], end_send.at[unit]).wait_send()
+
+
+def plan_of(out_rows, width):
     cut = out_rows // 4
     marks = [cut * index for index in range(5)]
     spans = list(zip(marks[:-1], marks[1:]))
@@ -534,7 +502,10 @@
         base += columns
     groups = [(low, high, (0, 1))]
     groups += [(start, stop, (number + 2,)) for number, (start, stop) in enumerate(spans[1:])]
-    return chunks, groups, base
+    middle = width // 512 * 256
+    units = [(number, 0, width) for number in range(len(groups) - 1)]
+    units += [(len(groups) - 1, 0, middle), (len(groups) - 1, middle, width)]
+    return chunks, groups, units, base
 
 
 def local_fused(layers, table, fitting, owner, local_slice, block_index, weight_index):
@@ -546,9 +517,8 @@
     owned = depth // points
     half = columns // 2
     out_rows = columns // peers
-    padded = -(-width // 128) * 128
     pairs = rows_dev // points
-    chunks, groups, held = plan_of(out_rows)
+    chunks, groups, units, held = plan_of(out_rows, width)
     bf16, f32 = jnp.bfloat16, jnp.float32
     dma = pltpu.SemaphoreType.DMA
 
@@ -559,7 +529,7 @@
             "core_out": pltpu.VMEM((4, slots, cols, points), bf16),
             "core_in": pltpu.VMEM((4, slots, cols, points), bf16),
             "row_out": pltpu.VMEM((3, slots, cols, points), bf16),
-            "row_in": pltpu.VMEM((5, slots, cols, points), bf16),
+            "row_in": pltpu.VMEM((4, slots, cols, points), bf16),
             "pieces": pltpu.VMEM((4, slots, cols, points), bf16),
         }
         if number > 0:
@@ -567,21 +537,24 @@
             refs["swap_in"] = pltpu.VMEM((pairs, cols, points), bf16)
         return refs
 
-    def group_scratch(number):
+    def unit_scratch(unit):
+        number, begins, ends = unit
         low, high, _ = groups[number]
+        padded = -(-(ends - begins) // 128) * 128
         return {
             "product": pltpu.VMEM((3, high - low, padded), bf16),
-            "landed": pltpu.VMEM((5, high - low, padded), bf16),
+            "landed": pltpu.VMEM((4, high - low, padded), bf16),
         }
 
     widest = max(chunk["columns"] for chunk in chunks[1:])
     tallest = max(4 * (high - low) for low, high, _ in groups)
-    any_space = pl.BlockSpec(memory_space=pl.ANY)
+    hbm = pl.BlockSpec(memory_space=pltpu.HBM)
+    vmem = pl.BlockSpec(memory_space=pltpu.VMEM)
     return pl.pallas_call(
-        functools.partial(fused_kernel, peers, owned, chunks, groups),
-        out_shape=jax.ShapeDtypeStruct((out_rows, width), bf16),
-        in_specs=[any_space] * 7,
-        out_specs=any_space,
+        functools.partial(fused_kernel, peers, owned, chunks, groups, units),
+        out_shape=pltpu.VMEM((out_rows, width), bf16),
+        in_specs=[hbm] * 7,
+        out_specs=vmem,
         scratch_shapes=[
             pltpu.VMEM((rows_dev, half), bf16),
             pltpu.VMEM((rows_dev, half), bf16),
@@ -599,20 +572,24 @@
             pltpu.SMEM((8, 128), jnp.int32),
             pltpu.VMEM((width, depth), bf16),
             pltpu.VMEM((tallest, depth), bf16),
-            pltpu.VMEM((columns, padded), f32),
+            pltpu.VMEM((columns, width), f32),
             pltpu.VMEM((owned // 2, held, points), f32),
-            pltpu.VMEM((out_rows, width), bf16),
             [chunk_scratch(number) for number in range(len(chunks))],
-            [group_scratch(number) for number in range(len(groups))],
-            dma((8 + len(groups),)),
-            dma((3, 1)),
+            [unit_scratch(unit) for unit in units],
+            dma((8,)),
+            dma((3,)),
+            dma((2, len(chunks) - 1)),
             dma((2, len(chunks))),
-            dma((2, len(chunks), 4)),
-            dma((2, len(chunks), 5)),
-            dma((2, len(chunks), 3)),
-            dma((2, len(groups), 5)),
+            dma((len(chunks),)),
+            dma((len(chunks), 3)),
+            dma((len(chunks),)),
+            dma((len(chunks),)),
+            dma((len(units),)),
+            dma((len(units), 3)),
         ],
-        compiler_params=pltpu.CompilerParams(collective_id=0, has_side_effects=True),
+        compiler_params=pltpu.CompilerParams(
+            collective_id=0, has_side_effects=True
+        ),
     )(
         layers[0],
         table.transpose(0, 2, 1),

time: 48.5 us -> 46.8 us (0.965)
  local copies, waits for them, and re-layouts: 1.63 us -> 0.69 us
  Pallas kernels: 46.7 us -> 46 us
    unnamed x1, local copies, waits for them, and re-layouts: 1.63 us -> 0.69 us
    pallas_call x1, Pallas kernels: 46.7 us -> 46 us  [local_fused(): pl.pallas_call(functools.partial(fused_kernel, peers, owned, chunks, grou...]
where the time goes in v4:
time: 46.8 us; the launch traced here: 46.7 us
  Pallas kernels  46 us (98%)
  local copies, waits for them, and re-layouts  0.69 us (1%)
    pallas_call x1, Pallas kernels, local_fused(): pl.pallas_call(functools.partial(fused_kernel, peers, owned, chunks, grou...  46 us

profile of v4, /device:TPU:0, one launch (start us, length us, event | category | flops | bytes accessed | tf_op | source)
XLA Modules:
  0.0 46.7 jit_solution(6317238365654318087)
XLA Ops:
  0.0 46.0 %shard_map.73 = bf16[64,1650]{1,0:T(8,128)(2,1)S(1)} custom-call(bf16[2048,256]{1,0:T(8,128)(2,1)} %bitcast.5, bf16[16,64,128]{2,1,0:T(8,128)(2,1)} %bitcast.6, s32[1,32]{1,0:T(1,128)} %bitcast.7, s32[1,32]{1,0:T(1,128)} %local_hbm.1, s32[1,32]{1,0:T(1,128)} %block_hbm.1, s32[1,32]{1,0:T(1,128)} %weight_hbm.1, bf16[1650,2048]{1,0:T(8,128)(2,1)} %bitcast.4), custom_call_target="tpu_custom_call" | custom-call | tf_op jit(solution)/shard_map/pallas_call | solution.py:553
  46.0 0.7 %copy.9 = bf16[64,1650]{1,0:T(8,128)(2,1)} copy(bf16[64,1650]{1,0:T(8,128)(2,1)S(1)} %shard_map.73) | data formatting | bytes 422400

commit v5 on v4

--- a/solution.py
+++ b/solution.py
@@ -125,6 +125,7 @@
     sibling = me + 1 - 2 * core
     order = (opposite, cross, mate, row)
     swapped = range(1, len(chunks))
+    late_chunks = (len(chunks) - 2, len(chunks) - 1)
 
     first_own = pl.multiple_of(side * half, half)
     first_other = pl.multiple_of((1 - side) * half, half)
@@ -271,8 +272,11 @@
                 def _():
                     row_copy(chunk, 2 + place, place, mate).start()
 
-            elif place == 2:
+            elif place == 2 and chunk not in late_chunks:
                 row_copy(chunk, 0, 2, mate).start()
+        if chunk == late_chunks[-1]:
+            for late in late_chunks:
+                row_copy(late, 0, 2, mate).start()
 
     def join(chunk, place):
         refs = chunk_refs[chunk]
@@ -286,15 +290,22 @@
             ).astype(jnp.bfloat16)
             row_copy(chunk, 1, place, order[place]).start()
 
-    def settle(chunk):
+    def settle(chunk, when=None):
         refs = chunk_refs[chunk]
-        all_of(refs["row_in"].at[0:2], row_recv.at[chunk, 0]).wait_recv()
-        value = own_part[:, rows_of(chunk), :]
-        for slot in range(2):
-            value = value + refs["row_in"][slot].astype(jnp.float32)
-        refs["pieces"][me] = value.astype(jnp.bfloat16)
-        for k in (1, 0, 2):
-            layer_copy(chunk, k).start()
+
+        def run():
+            all_of(refs["row_in"].at[0:2], row_recv.at[chunk, 0]).wait_recv()
+            value = own_part[:, rows_of(chunk), :]
+            for slot in range(2):
+                value = value + refs["row_in"][slot].astype(jnp.float32)
+            refs["pieces"][me] = value.astype(jnp.bfloat16)
+            for k in (1, 0, 2):
+                layer_copy(chunk, k).start()
+
+        if when is None:
+            run()
+        else:
+            pl.when(when)(run)
 
     def gather(number):
         low, high, members = groups[number]
@@ -336,39 +347,41 @@
         size = high - low
         return total[pl.ds(pl.multiple_of(4 * low + owner * size, size), size), begins:ends]
 
-    def deliver(unit):
+    def fill(unit):
         product = unit_refs[unit]["product"]
         _, begins, ends = units[unit]
         _, size, padded = product.shape
         if ends - begins < padded:
             product[:, :, padded - 128 :] = jnp.zeros((3, size, 128), jnp.bfloat16)
 
-        def fill(place):
+        def put(place):
             product[place, :, 0 : ends - begins] = total_of(unit, order[place]).astype(jnp.bfloat16)
 
+        for place in range(2):
+            pl.when(is_end)(functools.partial(put, place))
+        put(2)
+
+    def send_far(unit, place):
         @pl.when(is_end)
         def _():
-            for place in range(2):
-                fill(place)
-                end_copy(unit, 2 + place, place, mate).start()
-
-        fill(2)
+            end_copy(unit, 2 + place, place, mate).start()
+
+    def send_mate(unit):
         end_copy(unit, 0, 2, mate).start()
 
-    def pass_on(unit):
+    def pass_on(unit, place):
         product, landed = unit_refs[unit]["product"], unit_refs[unit]["landed"]
         _, begins, ends = units[unit]
         lanes = slice(0, ends - begins)
+        slot = 3 - place
 
         @pl.when(is_middle)
         def _():
-            for place in (1, 0):
-                slot = 3 - place
-                end_copy(unit, slot, place, mate).wait_recv()
-                product[place, :, lanes] = (
-                    total_of(unit, order[place]) + landed[slot, :, lanes].astype(jnp.float32)
-                ).astype(jnp.bfloat16)
-                end_copy(unit, 1, place, order[place]).start()
+            end_copy(unit, slot, place, mate).wait_recv()
+            product[place, :, lanes] = (
+                total_of(unit, order[place]) + landed[slot, :, lanes].astype(jnp.float32)
+            ).astype(jnp.bfloat16)
+            end_copy(unit, 1, place, order[place]).start()
 
     def finish(unit):
         landed = unit_refs[unit]["landed"]
@@ -429,48 +442,70 @@
     fit_copy.start()
     begin(2)
     share(2)
+    spread(2)
     join(1, 1)
-    spread(2)
     join(1, 0)
     begin(3)
     share(3)
     settle(0)
     spread(3)
     join(2, 1)
-    settle(1)
     begin(4)
     share(4)
     join(2, 0)
+    settle(1)
     spread(4)
     join(3, 1)
     settle(2)
+    join(3, 0)
+    join(4, 1)
+    join(4, 0)
     fit_copy.wait()
+    settle(3, is_middle)
     gather(0)
     multiply(0)
-    join(3, 0)
-    deliver(0)
-    join(4, 1)
-    join(4, 0)
-    settle(3)
+    fill(0)
+    send_far(0, 0)
+    send_far(0, 1)
+    send_mate(0)
+    settle(3, is_end)
+    settle(4, is_middle)
     gather(1)
     multiply(1)
-    deliver(1)
-    settle(4)
-    pass_on(0)
+    fill(1)
+    send_far(1, 0)
+    send_far(1, 1)
+    send_mate(1)
+    settle(4, is_end)
+    pass_on(0, 1)
+    pass_on(0, 0)
     gather(2)
     multiply(2)
-    deliver(2)
-    pass_on(1)
+    fill(2)
+    send_far(2, 0)
+    pass_on(1, 1)
+    pass_on(1, 0)
     gather(3)
     multiply(3)
-    deliver(3)
+    fill(3)
+    send_far(3, 0)
+    send_far(2, 1)
+    pass_on(2, 1)
     multiply(4)
-    deliver(4)
-    pass_on(2)
+    fill(4)
+    send_far(4, 0)
+    send_far(3, 1)
+    send_far(4, 1)
+    send_mate(2)
+    send_mate(3)
+    send_mate(4)
+    pass_on(3, 1)
     finish(0)
+    pass_on(2, 0)
+    pass_on(4, 1)
     finish(1)
-    pass_on(3)
-    pass_on(4)
+    pass_on(3, 0)
+    pass_on(4, 0)
     finish(2)
     finish(3)
     finish(4)

time: 46.8 us -> 45 us (0.962)
  Pallas kernels: 46 us -> 44.1 us
    pallas_call x1, Pallas kernels: 46 us -> 44.1 us  [local_fused(): pl.pallas_call(functools.partial(fused_kernel, peers, owned, chunks, grou...]
where the time goes in v5:
time: 45 us; the launch traced here: 44.8 us
  Pallas kernels  44.1 us (98%)
  local copies, waits for them, and re-layouts  0.69 us (2%)
    pallas_call x1, Pallas kernels, local_fused(): pl.pallas_call(functools.partial(fused_kernel, peers, owned, chunks, grou...  44.1 us

profile of v5, /device:TPU:0, one launch (start us, length us, event | category | flops | bytes accessed | tf_op | source)
XLA Modules:
  0.0 44.8 jit_solution(1135456680510820606)
XLA Ops:
  0.0 44.1 %shard_map.73 = bf16[64,1650]{1,0:T(8,128)(2,1)S(1)} custom-call(bf16[2048,256]{1,0:T(8,128)(2,1)} %bitcast.5, bf16[16,64,128]{2,1,0:T(8,128)(2,1)} %bitcast.6, s32[1,32]{1,0:T(1,128)} %bitcast.7, s32[1,32]{1,0:T(1,128)} %local_hbm.1, s32[1,32]{1,0:T(1,128)} %block_hbm.1, s32[1,32]{1,0:T(1,128)} %weight_hbm.1, bf16[1650,2048]{1,0:T(8,128)(2,1)} %bitcast.4), custom_call_target="tpu_custom_call" | custom-call | tf_op jit(solution)/shard_map/pallas_call | solution.py:588
  44.2 0.7 %copy.9 = bf16[64,1650]{1,0:T(8,128)(2,1)} copy(bf16[64,1650]{1,0:T(8,128)(2,1)S(1)} %shard_map.73) | data formatting | bytes 422400

commit v6 on v5

--- a/solution.py
+++ b/solution.py
@@ -113,7 +113,7 @@
     entries = owner_ref.shape[1]
     half_owned = owned // 2
     slices = peers * owned
-    step_entries = 8 if entries % 8 == 0 else 1
+    step_entries = next(size for size in (32, 16, 8, 1) if entries % size == 0)
     owner_width = half // 2
     mate = row + 1 - 2 * lax.rem(row, 2)
     cross = lax.rem(row + 2, peers)
@@ -206,10 +206,13 @@
 
         lax.fori_loop(0, entries // step_entries, body, 0)
 
-    def core_copy(chunk):
+    def core_copy(chunk, place):
         refs = chunk_refs[chunk]
-        sems = (core_sem.at[0, chunk], core_sem.at[1, chunk])
-        return remote(refs["core_out"], refs["core_in"], *sems, "layer", sibling)
+        source, target = refs["core_out"], refs["core_in"]
+        if chunk == 0:
+            source, target = source.at[place], target.at[place]
+        index = place if chunk == 0 else chunk + 3
+        return remote(source, target, core_sem.at[0, index], core_sem.at[1, index], "layer", sibling)
 
     def row_copy(chunk, slot, source, peer):
         refs = chunk_refs[chunk]
@@ -250,12 +253,14 @@
                 return carry
 
             lax.fori_loop(0, half_owned, body, 0, unroll=4)
-        core_copy(chunk).start()
+            if chunk == 0 or place == 3:
+                core_copy(chunk, place).start()
 
     def spread(chunk):
         refs = chunk_refs[chunk]
-        core_copy(chunk).wait_recv()
         for place, owner in enumerate(order):
+            if chunk == 0 or place == 0:
+                core_copy(chunk, place).wait_recv()
 
             def body(index, carry):
                 value = partial(chunk, owner, core, index) + refs["core_in"][place, index].astype(jnp.float32)
@@ -272,11 +277,18 @@
                 def _():
                     row_copy(chunk, 2 + place, place, mate).start()
 
-            elif place == 2 and chunk not in late_chunks:
-                row_copy(chunk, 0, 2, mate).start()
+            elif place == 2:
+
+                @pl.when(is_middle if chunk in late_chunks else True)
+                def _():
+                    row_copy(chunk, 0, 2, mate).start()
+
         if chunk == late_chunks[-1]:
-            for late in late_chunks:
-                row_copy(late, 0, 2, mate).start()
+
+            @pl.when(is_end)
+            def _():
+                for late in late_chunks:
+                    row_copy(late, 0, 2, mate).start()
 
     def join(chunk, place):
         refs = chunk_refs[chunk]
@@ -366,8 +378,10 @@
         def _():
             end_copy(unit, 2 + place, place, mate).start()
 
-    def send_mate(unit):
-        end_copy(unit, 0, 2, mate).start()
+    def send_mate(unit, when=True):
+        @pl.when(when)
+        def _():
+            end_copy(unit, 0, 2, mate).start()
 
     def pass_on(unit, place):
         product, landed = unit_refs[unit]["product"], unit_refs[unit]["landed"]
@@ -393,6 +407,9 @@
             value = value + landed[slot, :, 0 : ends - begins].astype(jnp.float32)
         result[low:high, begins:ends] = value.astype(result.dtype)
 
+    wide_table[...] = jnp.zeros_like(wide_table)
+    own_sums[0] = jnp.zeros(own_sums.shape[1:], own_sums.dtype)
+    got_sums[0] = jnp.zeros(got_sums.shape[1:], got_sums.dtype)
     for copy in small_copies:
         copy.wait()
     index_table(
@@ -416,21 +433,19 @@
         )
         for chunk in swapped
     }
-    for copy in swaps.values():
-        copy.start()
+    swaps[1].start()
     own_copy.wait()
     turn(own_raw, [(chunk, own_turned, chunks[chunk]["base"]) for chunk in swapped], side)
-    wide_table[...] = jnp.zeros_like(wide_table)
     table_copy.wait()
     for index in range(weights):
         wide_table[index, 0:block_rows, :] = turned_ref[index]
         wide_table[weights + index, block_rows:, :] = turned_ref[index]
-    own_sums[0] = jnp.zeros(own_sums.shape[1:], own_sums.dtype)
-    got_sums[0] = jnp.zeros(got_sums.shape[1:], got_sums.dtype)
     index_copy.wait()
     early_rows = chunks[0]["columns"]
     sum_terms(own_index, own_turned, own_sums, 0, early_rows)
     share(0)
+    for chunk in swapped[1:]:
+        swaps[chunk].start()
     spread(0)
     sum_terms(own_index, own_turned, own_sums, early_rows, own_turned.shape[1])
     meta_copy.wait_recv()
@@ -482,27 +497,30 @@
     gather(2)
     multiply(2)
     fill(2)
+    send_mate(2, is_middle)
     send_far(2, 0)
     pass_on(1, 1)
     pass_on(1, 0)
     gather(3)
     multiply(3)
     fill(3)
+    send_mate(3, is_middle)
     send_far(3, 0)
-    send_far(2, 1)
     pass_on(2, 1)
     multiply(4)
     fill(4)
+    send_mate(4, is_middle)
     send_far(4, 0)
+    send_far(2, 1)
     send_far(3, 1)
     send_far(4, 1)
-    send_mate(2)
-    send_mate(3)
-    send_mate(4)
+    send_mate(2, is_end)
+    send_mate(3, is_end)
+    send_mate(4, is_end)
     pass_on(3, 1)
+    pass_on(4, 1)
     finish(0)
     pass_on(2, 0)
-    pass_on(4, 1)
     finish(1)
     pass_on(3, 0)
     pass_on(4, 0)
@@ -514,7 +532,8 @@
     for copy in swaps.values():
         copy.wait_send()
     for chunk, refs in enumerate(chunk_refs):
-        core_copy(chunk).wait_send()
+        for place in range(4 if chunk == 0 else 1):
+            core_copy(chunk, place).wait_send()
         all_of(refs["row_out"], row_send.at[chunk]).wait_send()
         all_of(refs["pieces"].at[0:3], layer_send.at[chunk]).wait_send()
     for unit, refs in enumerate(unit_refs):
@@ -614,7 +633,7 @@
             dma((8,)),
             dma((3,)),
             dma((2, len(chunks) - 1)),
-            dma((2, len(chunks))),
+            dma((2, len(chunks) + 3)),
             dma((len(chunks),)),
             dma((len(chunks), 3)),
             dma((len(chunks),)),

time: 45 us -> 42.7 us (0.949)
  Pallas kernels: 44.1 us -> 41.8 us
    pallas_call x1, Pallas kernels: 44.1 us -> 41.8 us  [local_fused(): pl.pallas_call(functools.partial(fused_kernel, peers, owned, chunks, grou...]
where the time goes in v6:
time: 42.7 us; the launch traced here: 42.5 us
  Pallas kernels  41.8 us (98%)
  local copies, waits for them, and re-layouts  0.69 us (2%)
    pallas_call x1, Pallas kernels, local_fused(): pl.pallas_call(functools.partial(fused_kernel, peers, owned, chunks, grou...  41.8 us

profile of v6, /device:TPU:0, one launch (start us, length us, event | category | flops | bytes accessed | tf_op | source)
XLA Modules:
  0.0 42.5 jit_solution(10821666417586543862)
XLA Ops:
  0.0 41.8 %shard_map.73 = bf16[64,1650]{1,0:T(8,128)(2,1)S(1)} custom-call(bf16[2048,256]{1,0:T(8,128)(2,1)} %bitcast.5, bf16[16,64,128]{2,1,0:T(8,128)(2,1)} %bitcast.6, s32[1,32]{1,0:T(1,128)} %bitcast.7, s32[1,32]{1,0:T(1,128)} %local_hbm.1, s32[1,32]{1,0:T(1,128)} %block_hbm.1, s32[1,32]{1,0:T(1,128)} %weight_hbm.1, bf16[1650,2048]{1,0:T(8,128)(2,1)} %bitcast.4), custom_call_target="tpu_custom_call" | custom-call | tf_op jit(solution)/shard_map/pallas_call | solution.py:607
  41.8 0.7 %copy.9 = bf16[64,1650]{1,0:T(8,128)(2,1)} copy(bf16[64,1650]{1,0:T(8,128)(2,1)S(1)} %shard_map.73) | data formatting | bytes 422400

commit v7 on v6

--- a/solution.py
+++ b/solution.py
@@ -95,7 +95,7 @@
 
 
 def fused_kernel(
-    peers, owned, chunks, groups, units,
+    peers, owned, chunks, groups, units, split_chunks,
     layers_hbm, table_hbm, owner_hbm, local_hbm, block_hbm, weight_hbm, fitting_hbm, result,
     other_raw, own_raw, turned_ref, owner_ref, local_ref, block_ref, weight_ref,
     own_turned, wide_table, own_sums, got_sums, meta, own_index, got_index,
@@ -140,13 +140,22 @@
             )
         )
     ]
-    other_copy = pltpu.make_async_copy(layers_hbm.at[:, pl.ds(first_other, half)], other_raw, in_sem.at[0])
+    split_rows = other_raw.shape[0] // 2
+    other_copies = [
+        pltpu.make_async_copy(
+            layers_hbm.at[part * split_rows : (part + 1) * split_rows, pl.ds(first_other, half)],
+            other_raw.at[part * split_rows : (part + 1) * split_rows, :],
+            in_sem.at[8 * part],
+        )
+        for part in range(2)
+    ]
     own_copy = pltpu.make_async_copy(layers_hbm.at[:, pl.ds(first_own, half)], own_raw, in_sem.at[1])
     table_copy = pltpu.make_async_copy(table_hbm, turned_ref, in_sem.at[2])
     fit_copy = pltpu.make_async_copy(fitting_hbm, fit, in_sem.at[3])
     for copy in small_copies:
         copy.start()
-    other_copy.start()
+    for copy in other_copies:
+        copy.start()
     own_copy.start()
     table_copy.start()
 
@@ -169,9 +178,9 @@
     def all_of(ref, sem):
         return remote(ref, ref, sem, sem, "layer", partner)
 
-    def turn(raw, targets, early):
+    def turn(raw, targets, which, start_pair, stop_pair):
         low, high = chunks[0]["parts"][0][1:]
-        early_rows = pl.ds(pl.multiple_of(early * (high - low), high - low), high - low)
+        early_rows = pl.ds(pl.multiple_of(which * (high - low), high - low), high - low)
 
         def body(pair, carry):
             turned = raw[pl.ds(pl.multiple_of(pair * points, points), points), :].T
@@ -183,7 +192,7 @@
             own_turned[pair, early_rows, :] = turned[low:high]
             return carry
 
-        lax.fori_loop(0, pairs, body, 0, unroll=4)
+        lax.fori_loop(start_pair, stop_pair, body, 0, unroll=4)
 
     def sum_terms(index_ref, rows_ref, sums_ref, low, high):
         def body(step, carry):
@@ -209,9 +218,9 @@
     def core_copy(chunk, place):
         refs = chunk_refs[chunk]
         source, target = refs["core_out"], refs["core_in"]
-        if chunk == 0:
+        if chunk < split_chunks:
             source, target = source.at[place], target.at[place]
-        index = place if chunk == 0 else chunk + 3
+        index = 4 * chunk + place if chunk < split_chunks else chunk + 3 * split_chunks
         return remote(source, target, core_sem.at[0, index], core_sem.at[1, index], "layer", sibling)
 
     def row_copy(chunk, slot, source, peer):
@@ -253,13 +262,13 @@
                 return carry
 
             lax.fori_loop(0, half_owned, body, 0, unroll=4)
-            if chunk == 0 or place == 3:
-                core_copy(chunk, place).start()
+            if chunk < split_chunks or place == 3:
+                core_copy(chunk, place if chunk < split_chunks else 0).start()
 
     def spread(chunk):
         refs = chunk_refs[chunk]
         for place, owner in enumerate(order):
-            if chunk == 0 or place == 0:
+            if chunk < split_chunks or place == 0:
                 core_copy(chunk, place).wait_recv()
 
             def body(index, carry):
@@ -417,8 +426,10 @@
     )
     index_copy = pltpu.make_async_copy(meta, own_index, meta_sem.at[2])
     index_copy.start()
-    other_copy.wait()
-    turn(other_raw, [(chunk, chunk_refs[chunk]["swap_out"], 0) for chunk in swapped], 1 - side)
+    swap_targets = [(chunk, chunk_refs[chunk]["swap_out"], 0) for chunk in swapped]
+    for part, copy in enumerate(other_copies):
+        copy.wait()
+        turn(other_raw, swap_targets, 1 - side, part * pairs // 2, (part + 1) * pairs // 2)
     pl.semaphore_wait(barrier, 4 + 2 * lax.rem((row + 1) // 2, 2))
     meta_copy = remote(meta, got_index, meta_sem.at[0], meta_sem.at[1], "layer", partner)
     meta_copy.start()
@@ -435,7 +446,7 @@
     }
     swaps[1].start()
     own_copy.wait()
-    turn(own_raw, [(chunk, own_turned, chunks[chunk]["base"]) for chunk in swapped], side)
+    turn(own_raw, [(chunk, own_turned, chunks[chunk]["base"]) for chunk in swapped], side, 0, pairs)
     table_copy.wait()
     for index in range(weights):
         wide_table[index, 0:block_rows, :] = turned_ref[index]
@@ -444,18 +455,19 @@
     early_rows = chunks[0]["columns"]
     sum_terms(own_index, own_turned, own_sums, 0, early_rows)
     share(0)
-    for chunk in swapped[1:]:
-        swaps[chunk].start()
+    swaps[2].start()
     spread(0)
     sum_terms(own_index, own_turned, own_sums, early_rows, own_turned.shape[1])
     meta_copy.wait_recv()
     begin(1)
+    swaps[3].start()
     share(1)
     join(0, 1)
     spread(1)
     join(0, 0)
     fit_copy.start()
     begin(2)
+    swaps[4].start()
     share(2)
     spread(2)
     join(1, 1)
@@ -532,7 +544,7 @@
     for copy in swaps.values():
         copy.wait_send()
     for chunk, refs in enumerate(chunk_refs):
-        for place in range(4 if chunk == 0 else 1):
+        for place in range(4 if chunk < split_chunks else 1):
             core_copy(chunk, place).wait_send()
         all_of(refs["row_out"], row_send.at[chunk]).wait_send()
         all_of(refs["pieces"].at[0:3], layer_send.at[chunk]).wait_send()
@@ -556,7 +568,7 @@
         base += columns
     groups = [(low, high, (0, 1))]
     groups += [(start, stop, (number + 2,)) for number, (start, stop) in enumerate(spans[1:])]
-    middle = width // 512 * 256
+    middle = width * 3 // 1024 * 256
     units = [(number, 0, width) for number in range(len(groups) - 1)]
     units += [(len(groups) - 1, 0, middle), (len(groups) - 1, middle, width)]
     return chunks, groups, units, base
@@ -573,6 +585,7 @@
     out_rows = columns // peers
     pairs = rows_dev // points
     chunks, groups, units, held = plan_of(out_rows, width)
+    split_chunks = 1
     bf16, f32 = jnp.bfloat16, jnp.float32
     dma = pltpu.SemaphoreType.DMA
 
@@ -605,7 +618,7 @@
     hbm = pl.BlockSpec(memory_space=pltpu.HBM)
     vmem = pl.BlockSpec(memory_space=pltpu.VMEM)
     return pl.pallas_call(
-        functools.partial(fused_kernel, peers, owned, chunks, groups, units),
+        functools.partial(fused_kernel, peers, owned, chunks, groups, units, split_chunks),
         out_shape=pltpu.VMEM((out_rows, width), bf16),
         in_specs=[hbm] * 7,
         out_specs=vmem,
@@ -630,10 +643,10 @@
             pltpu.VMEM((owned // 2, held, points), f32),
             [chunk_scratch(number) for number in range(len(chunks))],
             [unit_scratch(unit) for unit in units],
-            dma((8,)),
+            dma((9,)),
             dma((3,)),
             dma((2, len(chunks) - 1)),
-            dma((2, len(chunks) + 3)),
+            dma((2, len(chunks) + 3 * split_chunks)),
             dma((len(chunks),)),
             dma((len(chunks), 3)),
             dma((len(chunks),)),

time: 42.7 us -> 42.4 us (level)
  no operation moved by 1% of the time
where the time goes in v7:
time: 42.4 us; the launch traced here: 42.1 us
  Pallas kernels  41.4 us (98%)
  local copies, waits for them, and re-layouts  0.69 us (2%)
    pallas_call x1, Pallas kernels, local_fused(): pl.pallas_call(functools.partial(fused_kernel, peers, owned, chunks, grou...  41.4 us

profile of v7, /device:TPU:0, one launch (start us, length us, event | category | flops | bytes accessed | tf_op | source)
XLA Modules:
  0.0 42.1 jit_solution(3633403276933795024)
XLA Ops:
  0.0 41.4 %shard_map.73 = bf16[64,1650]{1,0:T(8,128)(2,1)S(1)} custom-call(bf16[2048,256]{1,0:T(8,128)(2,1)} %bitcast.5, bf16[16,64,128]{2,1,0:T(8,128)(2,1)} %bitcast.6, s32[1,32]{1,0:T(1,128)} %bitcast.7, s32[1,32]{1,0:T(1,128)} %local_hbm.1, s32[1,32]{1,0:T(1,128)} %block_hbm.1, s32[1,32]{1,0:T(1,128)} %weight_hbm.1, bf16[1650,2048]{1,0:T(8,128)(2,1)} %bitcast.4), custom_call_target="tpu_custom_call" | custom-call | tf_op jit(solution)/shard_map/pallas_call | solution.py:620
  41.4 0.7 %copy.9 = bf16[64,1650]{1,0:T(8,128)(2,1)} copy(bf16[64,1650]{1,0:T(8,128)(2,1)S(1)} %shard_map.73) | data formatting | bytes 422400

commit v8 on v7

--- a/solution.py
+++ b/solution.py
@@ -350,9 +350,12 @@
                             target = (2 * far + part) * size
                             left[target : target + size, lanes] = value[place * size : (place + 1) * size]
 
-    def multiply(unit):
+    def multiply(unit, half=None):
         number, begins, ends = units[unit]
         low, high, _ = groups[number]
+        middle = begins + (ends - begins) // 512 * 256
+        if half is not None:
+            begins, ends = ((begins, middle), (middle, ends))[half]
         for start in range(begins, ends, 256):
             stop = min(start + 256, ends)
             total[4 * low : 4 * high, start:stop] = lax.dot_general(
@@ -485,20 +488,22 @@
     join(3, 1)
     settle(2)
     join(3, 0)
+    fit_copy.wait()
+    gather(0)
+    multiply(0, 0)
     join(4, 1)
+    multiply(0, 1)
     join(4, 0)
-    fit_copy.wait()
     settle(3, is_middle)
-    gather(0)
-    multiply(0)
     fill(0)
     send_far(0, 0)
     send_far(0, 1)
     send_mate(0)
     settle(3, is_end)
+    gather(1)
+    multiply(1, 0)
     settle(4, is_middle)
-    gather(1)
-    multiply(1)
+    multiply(1, 1)
     fill(1)
     send_far(1, 0)
     send_far(1, 1)

time: 42.4 us -> 42.4 us (level)
  no operation moved by 1% of the time
where the time goes in v8:
time: 42.4 us; the launch traced here: 42.1 us
  Pallas kernels  41.4 us (98%)
  local copies, waits for them, and re-layouts  0.69 us (2%)
    pallas_call x1, Pallas kernels, local_fused(): pl.pallas_call(functools.partial(fused_kernel, peers, owned, chunks, grou...  41.4 us

profile of v8, /device:TPU:0, one launch (start us, length us, event | category | flops | bytes accessed | tf_op | source)
XLA Modules:
  0.0 42.1 jit_solution(8861443252113403529)
XLA Ops:
  0.0 41.4 %shard_map.73 = bf16[64,1650]{1,0:T(8,128)(2,1)S(1)} custom-call(bf16[2048,256]{1,0:T(8,128)(2,1)} %bitcast.5, bf16[16,64,128]{2,1,0:T(8,128)(2,1)} %bitcast.6, s32[1,32]{1,0:T(1,128)} %bitcast.7, s32[1,32]{1,0:T(1,128)} %local_hbm.1, s32[1,32]{1,0:T(1,128)} %block_hbm.1, s32[1,32]{1,0:T(1,128)} %weight_hbm.1, bf16[1650,2048]{1,0:T(8,128)(2,1)} %bitcast.4), custom_call_target="tpu_custom_call" | custom-call | tf_op jit(solution)/shard_map/pallas_call | solution.py:625
  41.4 0.7 %copy.9 = bf16[64,1650]{1,0:T(8,128)(2,1)} copy(bf16[64,1650]{1,0:T(8,128)(2,1)S(1)} %shard_map.73) | data formatting | bytes 422400
